TPU v7x, 32 devices: a whole 2x2x4 slice. The times are simulated.
32 devices in a mesh: dp: 8 (over z, x), seq: 4 (over y, core).
Axes of the slice: x: 2, y: 2, z: 4, core: 2. Of those that a mesh axis runs over, the one named last changes fastest.
Arguments:
- layer_input: bfloat16 [20480, 768], P(('dp', 'seq')), may hold values from -6 to 6
- segment_ids: int32 [8, 2560], P('dp'), may hold values from 0 to 2, never falling along the last dimension, each value on 1 to 2048 neighbouring positions
- cotangent: bfloat16 [20480, 768], P(('dp', 'seq')), may hold values from -6 to 6
- attn_gain: bfloat16 [768], replicated, may hold values from 0.25 to 1.75
- attn_shift: bfloat16 [768], replicated, may hold values from -1.796875 to 1.796875
- query_weight: bfloat16 [768, 768], P(None, 'seq'), may hold values from -0.21875 to 0.21875
- query_bias: bfloat16 [768], P('seq'), may hold values from -1.796875 to 1.796875
- key_weight: bfloat16 [768, 768], P(None, 'seq'), may hold values from -0.21875 to 0.21875
- value_weight: bfloat16 [768, 768], P(None, 'seq'), may hold values from -0.21875 to 0.21875
- value_bias: bfloat16 [768], P('seq'), may hold values from -0.1796875 to 0.1796875
- out_weight: bfloat16 [768, 768], P('seq'), may hold values from -6 to 6
- out_bias: bfloat16 [768], replicated, may hold values from -1.796875 to 1.796875
- ffn_gain: bfloat16 [768], replicated, may hold values from 0.25 to 1.75
- ffn_shift: bfloat16 [768], replicated, may hold values from -1.796875 to 1.796875
- up_weight: bfloat16 [768, 3072], P(None, 'seq'), may hold values from -0.21875 to 0.21875
- up_bias: bfloat16 [3072], P('seq'), may hold values from -1.796875 to 1.796875
- down_weight: bfloat16 [3072, 768], P('seq'), may hold values from -0.109375 to 0.109375
- down_bias: bfloat16 [768], replicated, may hold values from -1.796875 to 1.796875
Outputs:
- layer_output: bfloat16 [20480, 768], P(('dp', 'seq'))
- input_grad: float32 [20480, 768], P(('dp', 'seq'))
- grad_attn_gain: float32 [768], replicated
- grad_attn_shift: float32 [768], replicated
- grad_query_weight: float32 [768, 768], P(None, 'seq')
- grad_query_bias: float32 [768], P('seq')
- grad_key_weight: float32 [768, 768], P(None, 'seq')
- grad_value_weight: float32 [768, 768], P(None, 'seq')
- grad_value_bias: float32 [768], P('seq')
- grad_out_weight: float32 [768, 768], P('seq')
- grad_out_bias: float32 [768], replicated
- grad_ffn_gain: float32 [768], replicated
- grad_ffn_shift: float32 [768], replicated
- grad_up_weight: float32 [768, 3072], P(None, 'seq')
- grad_up_bias: float32 [3072], P('seq')
- grad_down_weight: float32 [3072, 768], P('seq')
- grad_down_bias: float32 [768], replicated
Inputs may be any that keep to these rules, and one draw needn't show every extreme that they name: `segment_ids`: along a row the ids never fall; each of the 3 ids covers 1 to 2048 consecutive tokens, and some document has exactly 2048 tokens.
All inputs are finite; a program needn't handle non-finite values.
Results may differ from a plain program's by a relative error of at most 0.014.
Values may be sent and summed in bfloat16 or wider, within the bound.
A program may use at most 192 MiB of HBM per device.

v0:
```python
import functools

import jax
import jax.numpy as jnp
from jax import lax
from jax.experimental import pallas as pl
from jax.experimental.pallas import tpu as pltpu
from jax.sharding import PartitionSpec as P

HEAD = 64
SCALE = HEAD ** (-0.5)
LOG_SCALE = SCALE * 1.4426950408889634
LONGEST = 2048
EPSILON = 1e-06
NN = (((1,), (0,)), ((), ()))
NT = (((1,), (1,)), ((), ()))
TN = (((0,), (0,)), ((), ()))
MESH = pl.DeviceIdType.MESH
LOW = jnp.bfloat16
FULL = jnp.float32
VMEM = pl.BlockSpec(memory_space=pltpu.VMEM)
SMEM = pl.BlockSpec(memory_space=pltpu.SMEM)
ANY = pl.BlockSpec(memory_space=pl.ANY)
DMA = pltpu.SemaphoreType.DMA


def flip(index, bit):
    size = 1 << bit
    return index + size - 2 * size * lax.rem(lax.div(index, size), 2)


class Team:
    def __init__(self):
        self.row = lax.axis_index("dp")
        self.me = lax.axis_index("seq")
        self.sibling = flip(self.me, 0)
        self.far = flip(self.me, 1)
        self.diagonal = flip(self.sibling, 1)

    def device(self, index):
        return (self.row, index)

    def greet(self, others, *more):
        barrier = pltpu.get_barrier_semaphore()
        devices = [self.device(other) for other in others] + list(more)
        for device in devices:
            pl.semaphore_signal(barrier, inc=1, device_id=device, device_id_type=MESH)
        pl.semaphore_wait(barrier, len(devices))

    def copy(self, source, target, send, receive, other):
        return pltpu.make_async_remote_copy(
            src_ref=source,
            dst_ref=target,
            send_sem=send,
            recv_sem=receive,
            device_id=self.device(other),
            device_id_type=MESH,
        )


def rows_at(start, count, multiple):
    return pl.ds(pl.multiple_of(start, multiple), count)


def standardize(values):
    average = jnp.mean(values, axis=-1, keepdims=True)
    centered = values - average
    variance = jnp.mean(centered * centered, axis=-1, keepdims=True)
    inverse = lax.rsqrt(variance + EPSILON)
    return centered * inverse, inverse


def norm_back(grad, gain_row, standard, inverse):
    scaled = grad * gain_row
    mean_one = jnp.mean(scaled, axis=-1, keepdims=True)
    mean_two = jnp.mean(scaled * standard, axis=-1, keepdims=True)
    return inverse * (scaled - mean_one - standard * mean_two)


def column_sums(values):
    return jnp.sum(values, axis=0, keepdims=True)


def first_at_least(segments, value):
    length = segments.shape[1]

    def halve(unused, ends):
        low, high = ends
        middle = jnp.minimum(lax.div(low + high, 2), length - 1)
        below = segments[0, middle] < value
        open_yet = low < high
        return (
            jnp.where(open_yet & below, middle + 1, low),
            jnp.where(open_yet & jnp.logical_not(below), middle, high),
        )

    return lax.fori_loop(0, length.bit_length(), halve, (jnp.int32(0), jnp.int32(length)))[0]


def rotation(segments):
    length = segments.shape[1]
    one, two = first_at_least(segments, 1), first_at_least(segments, 2)
    offset = jnp.where(one == LONGEST, 0, jnp.where(two - one == LONGEST, one, two))
    border = jnp.where(one == LONGEST, two - one, jnp.where(two - one == LONGEST, length - two, one))
    return offset, border


def as_row(ref):
    return ref[...].astype(FULL).reshape(1, -1)


def dot(left_side, right_side, dims):
    return lax.dot_general(left_side, right_side, dims, preferred_element_type=jnp.float32)


def keep_head(head, values):
    lane = lax.broadcasted_iota(jnp.int32, values.shape, 1)
    inside = (lane >= head * HEAD) & (lane < (head + 1) * HEAD)
    return jnp.where(inside, values, jnp.zeros_like(values))


class Spread:
    def __init__(self, team, source, target, rows_of, sems):
        self.team, self.source, self.target, self.rows_of, self.sems = team, source, target, rows_of, sems

    def place(self, owner):
        return self.target.at[self.rows_of(owner)]

    def across(self):
        here = self.place(self.team.me)
        return self.team.copy(self.source, here, self.sems.at[0], self.sems.at[1], self.team.far)

    def near(self):
        here = self.place(self.team.me)
        return self.team.copy(self.source, here, self.sems.at[2], self.sems.at[3], self.team.sibling)

    def passed(self):
        there = self.place(self.team.far)
        return self.team.copy(there, there, self.sems.at[4], self.sems.at[5], self.team.sibling)

    def kept(self):
        return pltpu.make_async_copy(self.source, self.place(self.team.me), self.sems.at[6])

    def start(self):
        self.across().start()
        self.near().start()
        self.kept().start()

    def middle(self):
        self.across().wait_recv()
        self.passed().start()

    def sent(self):
        self.across().wait_send()
        self.near().wait_send()
        self.passed().wait_send()


EXTRA = 72


def rotated_block(ref, shift, length, index):
    width = ref.shape[2]
    sub = lax.broadcasted_iota(jnp.int32, (32, 8, width), 1)
    start = lax.rem(shift + index * 256, length)
    group = lax.div(start, 8)
    skip = start - group * 8
    turned = pltpu.roll(ref[pl.ds(group, 33)], lax.rem(8 - skip, 8), 1)
    return jnp.where(sub < 8 - skip, turned[:32], turned[1:]).reshape(256, width)


def rotate(ref, shift, length, put):
    def one(index, nothing):
        put(index, rotated_block(ref, shift, length, index))
        return nothing

    lax.fori_loop(0, length // 256, one, 0)


def wrap(ref, length):
    ref[length // 8 : length // 8 + EXTRA] = ref[0:EXTRA]


def rotate_into(source, target, buffer, shift):
    length, width = source.shape
    buffer[0 : length // 8] = source[...].astype(FULL).reshape(length // 8, 8, width)
    wrap(buffer, length)

    def put(index, block):
        target[rows_at(index * 256, 256, 256), :] = block.astype(LOW)

    rotate(buffer, shift, length, put)


def forward_kernel(
    rows_of,
    keys_of,
    head_count,
    spans,
    q_ref,
    k_ref,
    v_ref,
    wo_ref,
    mixed_ref,
    mixed_rot_ref,
    log_ref,
    pieces,
    wo_all,
    q_rot,
    k_rot,
    v_rot,
    v_heads,
    buffer,
    wo_sems,
    far_sems,
    near_sems,
    pass_sems,
):
    length, width = q_ref.shape
    team = Team()
    spread = Spread(team, wo_ref, wo_all, lambda owner: rows_at(owner * width, width, 64), wo_sems)

    def far_copy(index):
        rows = rows_at(index * 256, 256, 256)
        return team.copy(
            mixed_ref.at[rows], pieces.at[1, rows], far_sems.at[0, index], far_sems.at[1, index], team.far
        )

    def near_copy(index):
        rows = rows_at(index * 256, 256, 256)
        return team.copy(
            mixed_ref.at[rows], pieces.at[0, rows], near_sems.at[0, index], near_sems.at[1, index], team.sibling
        )

    def pass_copy(index):
        rows = rows_at(index * 256, 256, 256)
        return team.copy(
            pieces.at[1, rows], pieces.at[2, rows], pass_sems.at[0, index], pass_sems.at[1, index], team.sibling
        )

    team.greet((team.sibling, team.far))
    spread.start()
    small = length - LONGEST
    offset, border = rotation(spans)

    rotate_into(q_ref, q_rot, buffer, offset)
    rotate_into(k_ref, k_rot, buffer, offset)
    rotate_into(v_ref, v_rot, buffer, offset)
    v_all = v_rot[...]
    for head in range(head_count):
        v_heads[head] = jnp.concatenate(
            [keep_head(head, v_all), jnp.full((length, 256 - width), 1, jnp.bfloat16)], axis=1
        )

    def block(row, key_base, key_count, masked):
        rows = pl.ds(row, rows_of)
        total = jnp.zeros((rows_of, width), jnp.float32)
        logs = []
        for head in range(head_count):
            q_head = keep_head(head, q_rot[rows, :])
            top, parts = None, []
            for chunk in range(key_count // keys_of):
                keys = pl.ds(key_base + chunk * keys_of, keys_of)
                scores = dot(q_head, k_rot[keys, :], NT)
                if masked:
                    shape = (rows_of, keys_of)
                    row_id = lax.broadcasted_iota(jnp.int32, shape, 0) + (row - LONGEST)
                    key_id = lax.broadcasted_iota(jnp.int32, shape, 1) + chunk * keys_of
                    scores = jnp.where((row_id < border) == (key_id < border), scores, -1e30)
                high = jnp.max(scores, axis=1, keepdims=True)
                top = high if top is None else jnp.maximum(top, high)
                parts.append(scores)
            summed = jnp.zeros((rows_of, 256), jnp.float32)
            for chunk, scores in enumerate(parts):
                keys = pl.ds(key_base + chunk * keys_of, keys_of)
                weights = jnp.exp2((scores - top) * LOG_SCALE).astype(jnp.bfloat16)
                summed = summed + dot(weights, v_heads[head, keys, :], NN)
            norm = summed[:, 255:256]
            total = total + summed[:, :width] * (1.0 / norm)
            logs.append(top * LOG_SCALE + jnp.log2(norm))
        mixed_rot_ref[pl.ds(lax.div(row, 8), rows_of // 8)] = total.reshape(rows_of // 8, 8, width)
        logs.append(jnp.zeros((rows_of, 128 - head_count), jnp.float32))
        log_ref[rows, :] = jnp.concatenate(logs, axis=1)

    def send(index):
        rows = rows_at(index * 256, 256, 256)
        mixed_ref[rows, :] = rotated_block(mixed_rot_ref, length - offset, length, index).astype(LOW)
        far_copy(index).start()
        near_copy(index).start()

    def pass_on(index):
        far_copy(index).wait_recv()
        pass_copy(index).start()

    def little(index, nothing):
        block(pl.multiple_of(LONGEST + index * rows_of, rows_of), LONGEST, small, True)
        return nothing

    lax.fori_loop(0, small // rows_of, little, 0)
    lag, trips = 2, LONGEST // rows_of

    def large(index, nothing):
        block(pl.multiple_of(index * rows_of, rows_of), 0, LONGEST, False)

        @pl.when(index == 0)
        def _():
            mixed_rot_ref[length // 8 : length // 8 + 32] = mixed_rot_ref[0:32]

        send(index)

        @pl.when(index == trips // 2)
        def _():
            spread.middle()

        @pl.when(index >= lag)
        def _():
            pass_on(index - lag)

        return nothing

    lax.fori_loop(0, trips, large, 0)
    blocks = length // 256
    for index in range(trips, blocks):
        send(index)
    for index in range(trips - lag, blocks):
        pass_on(index)
    for index in range(blocks):
        near_copy(index).wait()
        far_copy(index).wait_send()
        pass_copy(index).wait()
    spread.sent()
    spread.near().wait_recv()
    spread.passed().wait_recv()
    spread.kept().wait()


def attend_forward(spans, queries, key_rows, value_rows, out_weight):
    length, width = queries.shape
    head_count = width // HEAD
    return pl.pallas_call(
        functools.partial(forward_kernel, 256, 512, head_count),
        out_shape=(
            jax.ShapeDtypeStruct((length, width), jnp.bfloat16),
            jax.ShapeDtypeStruct((length // 8 + EXTRA, 8, width), jnp.float32),
            jax.ShapeDtypeStruct((length, 128), jnp.float32),
            jax.ShapeDtypeStruct((3, length, width), LOW),
            jax.ShapeDtypeStruct((4 * out_weight.shape[0], out_weight.shape[1]), LOW),
            jax.ShapeDtypeStruct((length, width), LOW),
            jax.ShapeDtypeStruct((length, width), LOW),
            jax.ShapeDtypeStruct((length, width), LOW),
        ),
        in_specs=[SMEM, VMEM, VMEM, VMEM, VMEM],
        out_specs=(VMEM, VMEM, VMEM, ANY, ANY, VMEM, VMEM, VMEM),
        scratch_shapes=[
            pltpu.VMEM((head_count, length, 256), jnp.bfloat16),
            pltpu.VMEM((length // 8 + EXTRA, 8, width), FULL),
            DMA((7,)),
            DMA((2, length // 256)),
            DMA((2, length // 256)),
            DMA((2, length // 256)),
        ],
        compiler_params=pltpu.CompilerParams(
            collective_id=1, has_side_effects=True, vmem_limit_bytes=60 << 20
        ),
        name="attend_forward",
    )(spans, queries, key_rows, value_rows, out_weight)


class Plane:
    def __init__(self, size):
        self.me, self.lane = lax.axis_index("dp"), lax.axis_index("seq")
        self.size, self.bits = size, size.bit_length() - 1
        self.ranks = min(4, size // 2)
        self.side, self.rank = lax.rem(self.me, 2), lax.rem(lax.div(self.me, 2), self.ranks)
        self.extra = (size // 2 // self.ranks).bit_length() - 1

    def device(self, index):
        return (index, self.lane)

    def partner(self, bit):
        return self.device(flip(self.me, bit))

    def digit(self, bit):
        return lax.rem(lax.div(self.me, 1 << bit), 2)

    def other_rank(self, offset):
        return lax.rem(self.rank + offset, self.ranks)

    def ranked(self, offset):
        return self.device(self.me + 2 * (self.other_rank(offset) - self.rank))

    def remote(self, source, target, sems, index, device):
        return pltpu.make_async_remote_copy(
            src_ref=source,
            dst_ref=target,
            send_sem=sems.at[0, index],
            recv_sem=sems.at[1, index],
            device_id=device,
            device_id_type=MESH,
        )


class Halving:
    def __init__(self, plane, part, wire, first, sends, receives, sems):
        self.plane, self.part, self.wire, self.first = plane, part, wire, first
        self.sends, self.receives, self.sems = sends, receives, sems
        self.halvings, self.whole = halvings_of(plane.bits)
        self.stages = 2 * self.halvings + self.whole + 1
        half = part.shape[0]
        self.bases, self.sizes = [0], [half]
        for level in range(self.halvings):
            size = self.sizes[-1] // 2
            self.bases.append(self.bases[-1] + plane.digit(level + 1) * size)
            self.sizes.append(size)
        self.step = self.sizes[-1]
        self.shift = plane.side * half

    def inner(self, level):
        return rows_at(self.bases[level], self.sizes[level], self.step)

    def place(self, level):
        return rows_at(self.shift + self.bases[level], self.sizes[level], self.step)

    def copies(self, stage):
        plane = self.plane
        if stage < self.halvings + self.whole:
            return [
                plane.remote(self.sends[stage], self.receives[stage], self.sems, stage, plane.partner(stage + 1))
            ]
        level = 2 * self.halvings + self.whole - stage
        here = self.wire.at[self.place(level)]
        return [plane.remote(here, here, self.sems, stage, plane.partner(level))]

    def start(self, stage):
        if stage < self.halvings:
            size = self.sizes[stage + 1]
            first = self.bases[stage] + (1 - self.plane.digit(stage + 1)) * size
            self.sends[stage][...] = self.part[rows_at(first, size, self.step), :].astype(LOW)
        elif stage < self.halvings + self.whole:
            self.sends[stage][...] = self.part[self.inner(self.halvings), :].astype(LOW)
        elif stage == self.halvings + self.whole:
            self.wire[self.place(self.halvings), :] = self.part[self.inner(self.halvings), :].astype(LOW)
        for copy in self.copies(stage):
            copy.start()

    def finish(self, stage):
        for copy in self.copies(stage):
            copy.wait()
        if stage < self.halvings:
            self.part[self.inner(stage + 1), :] += self.receives[stage][...].astype(FULL)
        elif stage < self.halvings + self.whole:
            value = self.sends[stage][...].astype(FULL) + self.receives[stage][...].astype(FULL)
            self.part[self.inner(self.halvings), :] = value


def halvings_of(bits):
    halvings = min(bits - 1, 2)
    return halvings, bits - 1 - halvings


def halving_scratch(size, half, width):
    bits = size.bit_length() - 1
    halvings, whole = halvings_of(bits)
    shapes = [(half >> (stage + 1), width) for stage in range(halvings)] + [(half >> halvings, width)] * whole
    kinds = [pltpu.VMEM(dims, LOW) for dims in shapes]
    return [kinds, list(kinds), DMA((2, 2 * halvings + whole + 1))]


class Direct:
    first = 0

    def __init__(self, plane, source, wire, part, received, sends, receives, sems):
        self.plane, self.source, self.wire, self.part = plane, source, wire, part
        self.received, self.sends, self.receives, self.sems = received, sends, receives, sems
        self.half = source.shape[0] // 2
        self.piece = self.half // plane.ranks
        self.stages = 4 + plane.extra

    def side_rows(self, side):
        return rows_at(side * self.half, self.half, self.half)

    def rank_rows(self, rank):
        return rows_at(rank * self.piece, self.piece, self.piece)

    def own_rows(self):
        start = self.plane.side * self.half + self.plane.rank * self.piece
        return rows_at(start, self.piece, self.piece)

    def copies(self, stage):
        plane = self.plane
        if stage == 0:
            source = self.source.at[self.side_rows(1 - plane.side)]
            return [plane.remote(source, self.received, self.sems, 0, plane.partner(0))]
        if stage == self.stages - 1:
            here = self.wire.at[self.side_rows(plane.side)]
            return [plane.remote(here, here, self.sems, 1, plane.partner(0))]
        if 1 < stage < self.stages - 2:
            slot = plane.ranks + stage - 3
            index = 2 * plane.ranks + stage - 2
            device = plane.partner(plane.bits - plane.extra + stage - 2)
            return [plane.remote(self.sends.at[slot], self.receives.at[slot], self.sems, index, device)]
        copies = []
        for offset in range(1, plane.ranks):
            device = plane.ranked(offset)
            if stage == 1:
                slot = offset - 1
                copies.append(
                    plane.remote(self.sends.at[slot], self.receives.at[slot], self.sems, 1 + offset, device)
                )
            else:
                here = self.wire.at[self.own_rows()]
                copies.append(plane.remote(here, here, self.sems, plane.ranks + offset, device))
        return copies

    def start(self, stage):
        plane = self.plane
        if stage == 1:
            for offset in range(1, plane.ranks):
                rows = self.rank_rows(plane.other_rank(offset))
                self.sends[offset - 1] = self.part[rows, :].astype(LOW)
        elif 1 < stage < self.stages - 2:
            self.sends[plane.ranks + stage - 3] = self.part[self.rank_rows(plane.rank), :].astype(LOW)
        elif stage == self.stages - 2:
            self.wire[self.own_rows(), :] = self.part[self.rank_rows(plane.rank), :].astype(LOW)
        for copy in self.copies(stage):
            copy.start()

    def finish(self, stage):
        plane = self.plane
        for copy in self.copies(stage):
            copy.wait()
        if stage == 0:
            received = self.received[...].astype(FULL)
            self.part[...] = self.source[self.side_rows(plane.side), :].astype(FULL) + received
        elif stage == 1:
            value = self.part[self.rank_rows(plane.rank), :]
            for slot in range(plane.ranks - 1):
                value = value + self.receives[slot].astype(FULL)
            self.part[self.rank_rows(plane.rank), :] = value
        elif stage < self.stages - 2:
            slot = plane.ranks + stage - 3
            value = self.sends[slot].astype(FULL) + self.receives[slot].astype(FULL)
            self.part[self.rank_rows(plane.rank), :] = value


def direct_scratch(size, rows, width):
    ranks = min(4, size // 2)
    extra = (size // 2 // ranks).bit_length() - 1
    half = rows // 2
    pieces = pltpu.VMEM((ranks - 1 + extra, half // ranks, width), LOW)
    return [
        pltpu.VMEM((half, width), FULL),
        pltpu.VMEM((half, width), LOW),
        pieces,
        pieces,
        DMA((2, 2 * ranks + extra)),
    ]


class Events:
    def __init__(self, totals):
        self.totals = totals
        last = totals[0].stages - 1
        self.waiting = sorted(
            (2 * (stage - total.first) + index, index, stage)
            for index, total in enumerate(totals)
            for stage in range(total.first, last)
        )

    def start(self):
        for total in self.totals:
            total.start(total.first)

    def take(self, limit):
        ready = [event for event in self.waiting if event[0] < limit]
        self.waiting = [event for event in self.waiting if event[0] >= limit]
        for unused, index, stage in ready:
            self.totals[index].finish(stage)
            self.totals[index].start(stage + 1)

    def next(self, count):
        if self.waiting[:count]:
            self.take(self.waiting[min(count, len(self.waiting)) - 1][0] + 1)

    def end(self):
        self.take(1 << 20)
        for total in self.totals:
            total.finish(total.stages - 1)


def greet_all(team, plane, direct):
    barrier = pltpu.get_barrier_semaphore()
    others = [plane.partner(bit) for bit in range(plane.bits)]
    others += [team.device(team.sibling), team.device(team.far)]
    greeted = list(others)
    if direct:
        greeted = [plane.partner(0), team.device(team.sibling), team.device(team.far)]
        greeted += [plane.partner(plane.bits - plane.extra + index) for index in range(plane.extra)]
        greeted += [plane.ranked(offset) for offset in range(1, plane.ranks)]
    for other in greeted:
        pl.semaphore_signal(barrier, inc=1, device_id=other, device_id_type=MESH)
    pl.semaphore_wait(barrier, len(greeted))
    return others


def backward_kernel(
    keys_of,
    rows_of,
    head_count,
    size,
    spans,
    q_rot,
    k_rot,
    v_rot,
    d_ref,
    mixed_rot_ref,
    log_ref,
    up_part,
    down_part,
    wo_part,
    out_far,
    dq_ref,
    dk_ref,
    dv_ref,
    up_sum,
    down_sum,
    wo_sum,
    out_in,
    d_rot,
    q_turned,
    d_turned,
    k_turned,
    q_heads,
    d_heads,
    dq_turned,
    dk_rot,
    dv_rot,
    log_rows,
    deltas,
    parts,
    wires,
    total_parts,
    wo_near,
    wo_far,
    wo_sems,
    out_sems,
    keep_sems,
    dq_side,
):
    length, width = q_rot.shape
    small = length - LONGEST
    offset, border = rotation(spans)
    low, full = jnp.bfloat16, jnp.float32
    team, plane = Team(), Plane(size)
    columns = wo_sum.shape[0]
    lanes_of = up_part.shape[1] // 2
    totals, loads = [], []
    for index, source in enumerate((up_part, up_part, down_part, down_part)):
        lanes = pl.ds((index % 2) * lanes_of, lanes_of)
        total = Halving(plane, parts.at[index], wires.at[index], index // 2 * 2, *total_parts[index])
        place = parts.at[index, total.inner(index // 2 * 2)]
        loads.append(pltpu.make_async_copy(source.at[:, lanes], place, keep_sems.at[index]))
        totals.append(total)
    for load in loads:
        load.start()
    events = Events(totals)
    greet_all(team, plane, False)
    for load in loads:
        load.wait()
    events.start()
    out_copy = team.copy(out_far, out_in, out_sems.at[0], out_sems.at[1], team.far)
    out_copy.start()

    def wo_rows(owner):
        return rows_at(owner * columns, columns, 64)

    wo_copies = [
        team.copy(wo_part.at[wo_rows(owner)], wo_near.at[slot], wo_sems.at[0, slot], wo_sems.at[1, slot], team.sibling)
        for slot, owner in enumerate((team.sibling, team.diagonal))
    ]
    for copy in wo_copies:
        copy.start()
    wo_across = team.copy(wo_far.at[0], wo_far.at[1], wo_sems.at[0, 2], wo_sems.at[1, 2], team.far)

    rotate_into(d_ref, d_rot, dq_turned, offset)
    q_all, k_all, d_all = q_rot[...], k_rot[...], d_rot[...]
    q_turned[...] = jnp.transpose(q_all)
    k_turned[...] = jnp.transpose(k_all)
    d_turned[...] = jnp.transpose(d_all)
    for head in range(head_count):
        q_heads[head] = keep_head(head, q_all)
        d_heads[head] = keep_head(head, d_all)
    products = jnp.transpose(d_all.astype(full) * mixed_rot_ref[0 : length // 8].reshape(length, width))
    for head in range(head_count):
        deltas[head : head + 1, :] = jnp.sum(products[head * HEAD : (head + 1) * HEAD, :], axis=0, keepdims=True)
    log_rows[...] = jnp.transpose(log_ref[...])[0:8, :]
    dq_side[...] = jnp.zeros_like(dq_side)

    def block(key_row, row_base, row_count, masked, before):
        keys = pl.ds(key_row, keys_of)
        dk_sum = jnp.zeros((keys_of, width), full)
        dv_sum = jnp.zeros((keys_of, width), full)
        for head in range(head_count):
            before(head)
            k_head = keep_head(head, k_rot[keys, :])
            v_head = keep_head(head, v_rot[keys, :])
            lanes = slice(head * HEAD, (head + 1) * HEAD)
            k_side = k_turned[lanes, keys]
            for chunk in range(row_count // rows_of):
                start = row_base + chunk * rows_of
                rows = slice(start, start + rows_of)
                scores = dot(k_head, q_turned[:, rows], NN)
                dprobs = dot(v_head, d_turned[:, rows], NN)
                probs = jnp.exp2(scores * LOG_SCALE - log_rows[head : head + 1, rows])
                if masked:
                    shape = (keys_of, rows_of)
                    key_id = lax.broadcasted_iota(jnp.int32, shape, 0) + (key_row - LONGEST)
                    row_id = lax.broadcasted_iota(jnp.int32, shape, 1) + chunk * rows_of
                    probs = jnp.where((row_id < border) == (key_id < border), probs, 0.0)
                dv_sum = dv_sum + dot(probs.astype(low), d_heads[head, rows, :], NN)
                draw = (probs * (dprobs - deltas[head : head + 1, rows])).astype(low)
                dk_sum = dk_sum + dot(draw, q_heads[head, rows, :], NN)
                dq_side[lanes, rows] += dot(k_side, draw, NN)
        groups = pl.ds(lax.div(key_row, 8), keys_of // 8)
        dk_rot[groups] = (dk_sum * SCALE).reshape(keys_of // 8, 8, width)
        dv_rot[groups] = dv_sum.reshape(keys_of // 8, 8, width)

    trips = LONGEST // keys_of

    def gather_wo():
        for copy in wo_copies:
            copy.wait()
        wo_far[0] = (wo_part[wo_rows(team.far), :].astype(full) + wo_near[1].astype(full)).astype(low)
        wo_across.start()

    def large(index, nothing):
        def before(head):
            for trip in range(trips):
                slot = trip * head_count + head
                limit = (slot + 1) // 2
                earlier = slot // 2
                if limit > earlier:

                    @pl.when(index == trip)
                    def _(limit=limit, slot=slot):
                        events.waiting = [event for event in everything if event[0] >= earlier]
                        events.take(limit)
                        if slot == 1:
                            gather_wo()

        block(pl.multiple_of(index * keys_of, keys_of), 0, LONGEST, False, before)
        return nothing

    def little(index, nothing):
        block(
            pl.multiple_of(LONGEST + index * keys_of, keys_of), LONGEST, small, True, lambda head: None
        )
        return nothing

    everything = list(events.waiting)
    lax.fori_loop(0, trips, large, 0)
    slots = trips * head_count
    events.waiting = [event for event in everything if event[0] >= slots // 2]
    lax.fori_loop(0, small // keys_of, little, 0)

    def unrotate(buffer, target):
        wrap(buffer, length)

        def put(index, block_rows):
            target[rows_at(index * 256, 256, 256), :] = block_rows.astype(low)

        rotate(buffer, length - offset, length, put)

    unrotate(dk_rot, dk_ref)
    unrotate(dv_rot, dv_ref)
    dq_turned[0 : length // 8] = jnp.transpose(dq_side[...] * SCALE).reshape(length // 8, 8, width)
    unrotate(dq_turned, dq_ref)
    events.end()
    keeps = []
    for index, target in enumerate((up_sum, up_sum, down_sum, down_sum)):
        lanes = pl.ds((index % 2) * lanes_of, lanes_of)
        keeps.append(pltpu.make_async_copy(wires.at[index], target.at[:, lanes], keep_sems.at[index]))
    for keep in keeps:
        keep.start()
    wo_across.wait()
    mine = wo_part[wo_rows(team.me), :].astype(full) + wo_near[0].astype(full)
    wo_sum[...] = (mine + wo_far[1].astype(full)).astype(low)
    out_copy.wait()
    for keep in keeps:
        keep.wait()


def attend_backward(
    size, spans, q_rot, k_rot, v_rot, grad_mixed, mixed_rot, log_totals, up_part, down_part, wo_part, out_far
):
    length, width = q_rot.shape
    head_count = width // HEAD
    low, full = jnp.bfloat16, jnp.float32
    half = (up_part.shape[0], up_part.shape[1] // 2)
    whole = (2 * up_part.shape[0], up_part.shape[1])
    wo_shape = (wo_part.shape[0] // 4, wo_part.shape[1])

    def shape(dims):
        return jax.ShapeDtypeStruct(dims, low)

    grouped = (length // 8 + EXTRA, 8, width)
    return pl.pallas_call(
        functools.partial(backward_kernel, 256, 512, head_count, size),
        out_shape=(shape((length, width)),) * 3
        + (shape(whole), shape(whole), shape(wo_shape), shape(out_far.shape)),
        in_specs=[SMEM] + [VMEM] * 6 + [ANY, ANY, VMEM, ANY],
        out_specs=(VMEM,) * 3 + (ANY, ANY, VMEM, ANY),
        scratch_shapes=[
            pltpu.VMEM((length, width), low),
            pltpu.VMEM((width, length), low),
            pltpu.VMEM((width, length), low),
            pltpu.VMEM((width, length), low),
            pltpu.VMEM((head_count, length, width), low),
            pltpu.VMEM((head_count, length, width), low),
            pltpu.VMEM(grouped, full),
            pltpu.VMEM(grouped, full),
            pltpu.VMEM(grouped, full),
            pltpu.VMEM((8, length), full),
            pltpu.VMEM((8, length), full),
            pltpu.VMEM((4, *half), full),
            pltpu.VMEM((4, 2 * half[0], half[1]), low),
            [halving_scratch(size, *half) for unused in range(4)],
            pltpu.VMEM((2, *wo_shape), low),
            pltpu.VMEM((2, *wo_shape), low),
            DMA((2, 3)),
            DMA((2,)),
            DMA((4,)),
            pltpu.VMEM((width, length), full),
        ],
        compiler_params=pltpu.CompilerParams(
            collective_id=3, has_side_effects=True, vmem_limit_bytes=63 << 20
        ),
        name="attend_backward",
    )(spans, q_rot, k_rot, v_rot, grad_mixed, mixed_rot, log_totals, up_part, down_part, wo_part, out_far)


def project_kernel(
    part,
    x_ref,
    gain,
    shift,
    wq,
    bq,
    wk,
    wv,
    bv,
    x_all,
    normed,
    q_ref,
    k_ref,
    v_ref,
    landing,
    far_send,
    far_recv,
    near_send,
    near_recv,
    pass_send,
    pass_recv,
    keep_sem,
):
    team = Team()
    own = x_ref.shape[0]
    count = own // part

    def piece(owner, index):
        return rows_at(owner * own + index * part, part, part)

    def far_copy(index):
        source = x_ref.at[rows_at(index * part, part, part)]
        return team.copy(
            source, landing.at[piece(team.me, index)], far_send.at[index], far_recv.at[index], team.far
        )

    def pass_copy(index):
        place = landing.at[piece(team.far, index)]
        return team.copy(place, place, pass_send.at[index], pass_recv.at[index], team.sibling)

    near = team.copy(
        x_ref, landing.at[rows_at(team.me * own, own, own)], near_send, near_recv, team.sibling
    )

    def keep(owner, source, slot):
        return pltpu.make_async_copy(source, x_all.at[rows_at(owner * own, own, own)], keep_sem.at[slot])

    team.greet((team.sibling, team.far))
    for index in range(count):
        far_copy(index).start()
    near.start()
    keep(team.me, x_ref, 0).start()

    gain_row, shift_row, bq_row, bv_row = as_row(gain), as_row(shift), as_row(bq), as_row(bv)

    def project(owner, index, values):
        standard, unused = standardize(values.astype(FULL))
        low = (standard * gain_row + shift_row).astype(LOW)
        rows = piece(owner, index)
        normed[rows, :] = low
        q_ref[rows, :] = (dot(low, wq[...], NT) + bq_row).astype(LOW)
        k_ref[rows, :] = dot(low, wk[...], NT).astype(LOW)
        v_ref[rows, :] = (dot(low, wv[...], NT) + bv_row).astype(LOW)

    def mine(index, nothing):
        project(team.me, index, x_ref[rows_at(index * part, part, part), :])
        return nothing

    lax.fori_loop(0, count, mine, 0)
    near.wait()

    def next_to(index, nothing):
        project(team.sibling, index, landing[piece(team.sibling, index), :])
        return nothing

    lax.fori_loop(0, count, next_to, 0)

    def across(index, nothing):
        far_copy(index).wait_recv()
        pass_copy(index).start()
        project(team.far, index, landing[piece(team.far, index), :])
        pass_copy(index).wait_recv()
        project(team.diagonal, index, landing[piece(team.diagonal, index), :])
        return nothing

    lax.fori_loop(0, count, across, 0)
    for slot, owner in ((1, team.sibling), (2, team.far), (3, team.diagonal)):
        keep(owner, landing.at[rows_at(owner * own, own, own)], slot).start()
    for slot, owner in ((1, team.sibling), (2, team.far), (3, team.diagonal)):
        keep(owner, landing.at[rows_at(owner * own, own, own)], slot).wait()
    keep(team.me, x_ref, 0).wait()
    for index in range(count):
        far_copy(index).wait_send()
        pass_copy(index).wait_send()


def gather_and_project(x, gain, shift, wq, bq, wk, wv, bv):
    own, width = x.shape
    length, columns, part = 4 * own, wq.shape[0], 128
    count = own // part
    narrow = jax.ShapeDtypeStruct((length, columns), LOW)
    wide = jax.ShapeDtypeStruct((length, width), LOW)
    return pl.pallas_call(
        functools.partial(project_kernel, part),
        out_shape=(wide, wide, narrow, narrow, narrow),
        in_specs=[VMEM] * 8,
        out_specs=(ANY, VMEM, VMEM, VMEM, VMEM),
        scratch_shapes=[
            pltpu.VMEM((length, width), LOW),
            DMA((count,)),
            DMA((count,)),
            DMA,
            DMA,
            DMA((count,)),
            DMA((count,)),
            DMA((4,)),
        ],
        compiler_params=pltpu.CompilerParams(
            collective_id=0, has_side_effects=True, vmem_limit_bytes=48 << 20
        ),
        name="gather_and_project",
    )(x, gain, shift, wq, bq, wk, wv, bv)


class Reduction:
    def __init__(self, team, near_out, near_in, far_out, far_in, sems):
        self.team = team
        self.near_out, self.near_in, self.far_out, self.far_in = near_out, near_in, far_out, far_in
        self.sems = sems

    def near(self, pair):
        return self.team.copy(
            self.near_out.at[pair % 2],
            self.near_in.at[pair],
            self.sems.at[0, pair],
            self.sems.at[1, pair],
            self.team.sibling,
        )

    def across(self, pair):
        return self.team.copy(
            self.far_out.at[pair], self.far_in.at[pair], self.sems.at[2, pair], self.sems.at[3, pair], self.team.far
        )

    def give(self, pair, values):
        @pl.when(pair >= 2)
        def _():
            self.near(pair - 2).wait_send()

        self.near_out[pair % 2] = values.astype(LOW)
        self.near(pair).start()

    def combine(self, pair, values):
        self.near(pair).wait_recv()
        return values + self.near_in[pair].astype(FULL)

    def send(self, pair, values):
        self.far_out[pair] = values.astype(LOW)
        self.across(pair).start()

    def arrived(self, pair):
        self.across(pair).wait_recv()
        return self.far_in[pair].astype(FULL)

    def finish(self, pairs):
        for pair in range(pairs // 2):
            self.across(pair).wait_send()
        for pair in (pairs - 2, pairs - 1):
            self.near(pair).wait_send()


def owner_at(team_me, step):
    half = lax.div(step, 4)
    odd = lax.rem(step, 2)
    one = flip(team_me, 0)
    base = one + odd * (team_me - one)
    return lax.rem(base + 2 * (1 - half), 4)


def part_at(step):
    return lax.rem(lax.div(step, 2), 2)


def ffn_kernel(
    part,
    size,
    mixed_ref,
    pieces,
    x_all,
    cot_ref,
    wo,
    up,
    down,
    up_bias,
    out_bias,
    gain,
    shift,
    down_bias,
    out_far,
    out_own,
    grad_middle,
    grad_mixed,
    up_part,
    down_part,
    grad_wo,
    sums,
    middle_own,
    up_half,
    down_half,
    halves_out,
    halves_in,
    half_sems,
    halving_parts,
    keep_sems,
    cot_all,
    normed_all,
    hidden_all,
    gpre_all,
    out_slots,
    out_near,
    own_sum,
    near_out,
    near_in,
    far_out,
    far_in,
    mixed_out,
    branch_own,
    cot_sems,
    slot_sems,
    red_sems,
    a2a_sems,
):
    team = Team()
    length = mixed_ref.shape[0]
    width = x_all.shape[1]
    columns = mixed_ref.shape[1]
    own = length // 4
    steps = length // part

    def rows_of(owner, index):
        return rows_at(owner * own + index * part, part, part)

    def step_rows(device, step):
        return rows_of(owner_at(device, step), part_at(step))

    spreads = [
        Spread(
            team,
            cot_ref.at[pl.ds(index * part, part)],
            cot_all,
            lambda owner, index=index: rows_of(owner, index),
            cot_sems.at[index],
        )
        for index in range(own // part)
    ]
    reduction = Reduction(team, near_out, near_in, far_out, far_in, red_sems)

    def slot_copy(pair):
        slot = lax.rem(pair, 2)
        return team.copy(
            out_slots.at[slot], out_near.at[pair], slot_sems.at[0, slot], slot_sems.at[1, pair], team.sibling
        )

    plane = Plane(size)
    team.greet((team.sibling, team.far, team.diagonal), *[plane.partner(bit) for bit in range(3)])

    for spread in spreads:
        spread.start()
    sums[...] = jnp.zeros_like(sums)
    gain_row, shift_row, bias_row = as_row(gain), as_row(shift), as_row(out_bias)
    up_row, down_row = as_row(up_bias), as_row(down_bias)

    def forward(step, keep_middle):
        rows = step_rows(team.me, step)

        def weights(owner):
            return wo[rows_at(owner * columns, columns, 64), :]

        branch = dot(mixed_ref[rows, :], weights(team.me), NN)
        branch = branch + dot(pieces[0, rows, :], weights(team.sibling), NN)
        branch = branch + dot(pieces[1, rows, :], weights(team.far), NN)
        branch = branch + dot(pieces[2, rows, :], weights(team.diagonal), NN)
        middle = x_all[rows, :].astype(FULL) + (branch + bias_row)
        if keep_middle:

            @pl.when(step >= steps // 2)
            def _():
                middle_own[rows_at(part_at(step) * part, part, part), :] = middle

        standard, unused = standardize(middle)
        low = (standard * gain_row + shift_row).astype(LOW)
        normed_all[rows, :] = low
        pre = dot(low, up[...], NN) + up_row
        bell = 0.5 * (1.0 + lax.erf(pre * 0.7071067811865476))
        hidden = (pre * bell).astype(LOW)
        hidden_all[rows, :] = hidden
        slope = bell + pre * (jnp.exp(pre * pre * -0.5) * 0.3989422804014327)
        gpre_all[rows, :] = slope.astype(LOW)

        out = dot(hidden, down[...], NN)
        pair = lax.div(step, 2)
        if keep_middle:
            place = rows_at(part_at(step) * part, part, part)

            @pl.when(step < steps // 2)
            def _():
                out_far[place, :] = out.astype(LOW)

            @pl.when(step >= steps // 2)
            def _():
                out_own[place, :] = middle + out + down_row
        else:

            @pl.when(pair >= 2)
            def _():
                slot_copy(pair - 2).wait_send()

            out_slots[lax.rem(pair, 2)] = out.astype(LOW)
            slot_copy(pair).start()
    def backward(step):
        rows = step_rows(team.me, step)
        slope = gpre_all[rows, :].astype(FULL)
        grad_pre = (dot(cot_all[rows, :], down[...], NT) * slope).astype(LOW)
        gpre_all[rows, :] = grad_pre
        sums[4:5, :] += column_sums(grad_pre.astype(FULL))
        return dot(grad_pre, up[...], NT)

    def pair_forward(pair, nothing):
        forward(2 * pair, False)
        forward(2 * pair + 1, True)
        return nothing

    half = width // 2
    down_total = Halving(plane, down_half, None, 0, *halving_parts)
    up_keep = pltpu.make_async_copy(up_half, up_part, keep_sems.at[0])
    down_keep = pltpu.make_async_copy(down_half.at[down_total.inner(2)], down_part, keep_sems.at[1])
    halves = (normed_all, gpre_all, up_half), (hidden_all, cot_all, down_half)
    side_copies = [
        plane.remote(halves_out.at[index], halves_in.at[index], half_sems, index, plane.partner(0))
        for index in range(2)
    ]
    def place_of(pair):
        return rows_at(part_at(2 * pair) * part, part, part)

    def add_out(pair):
        slot_copy(pair).wait_recv()
        place, given = place_of(pair), out_near[pair].astype(FULL)

        @pl.when(pair < steps // 4)
        def _():
            out_far[place, :] = (out_far[place, :].astype(FULL) + given).astype(LOW)

        @pl.when(pair >= steps // 4)
        def _():
            out_own[place, :] += given

    def combine(pair):
        reduction.near(pair).wait_recv()
        given = reduction.near_in[pair].astype(FULL)

        @pl.when(pair < steps // 4)
        def _():
            reduction.send(pair, reduction.far_out[lax.rem(pair, 2)].astype(FULL) + given)

        @pl.when(pair >= steps // 4)
        def _():
            own_sum[place_of(pair), :] += given

    def pair_backward(pair, nothing):
        first, second = 2 * pair, 2 * pair + 1
        for index, spread in enumerate(spreads):

            @pl.when(pair == index)
            def _(spread=spread):
                spread.middle()
                spread.passed().wait_recv()

        @pl.when(pair == len(spreads))
        def _():
            for spread in spreads:
                spread.near().wait_recv()
                spread.kept().wait()
            side_half(1)

        @pl.when(pair == len(spreads) + 1)
        def _():
            own_half(1)

        reduction.give(pair, backward(first))
        add_out(pair)

        @pl.when(pair >= 1)
        def _():
            combine(pair - 1)

        values = backward(second)

        @pl.when(pair < steps // 4)
        def _():
            far_out[lax.rem(pair, 2)] = values.astype(LOW)

        @pl.when(pair >= steps // 4)
        def _():
            own_sum[place_of(pair), :] = values

        return nothing

    def side_half(index):
        left, right, unused = halves[index]
        lanes = rows_at((1 - plane.side) * half, half, half)

        def one(slab, nothing):
            columns_of = rows_at(slab * 256, 256, 256)
            halves_out[index, :, columns_of] = dot(left[:, lanes], right[:, columns_of], TN).astype(LOW)
            return nothing

        lax.fori_loop(0, width // 256, one, 0)
        side_copies[index].start()

    def own_half(index):
        left, right, target = halves[index]
        lanes = rows_at(plane.side * half, half, half)

        def one(slab, nothing):
            columns_of = rows_at(slab * 256, 256, 256)
            target[:, columns_of] = dot(left[:, lanes], right[:, columns_of], TN)
            return nothing

        lax.fori_loop(0, width // 256, one, 0)

    def add_side(index):
        side_copies[index].wait()
        halves[index][2][...] += halves_in[index].astype(FULL)

    lax.fori_loop(0, steps // 2, pair_forward, 0)
    lax.fori_loop(0, steps // 2, pair_backward, 0)
    side_half(0)
    add_side(1)
    down_total.start(0)
    combine(steps // 2 - 1)

    def back(index, nothing):
        @pl.when(index == 1)
        def _():
            down_total.finish(0)
            down_total.start(1)

        rows = rows_at(index * part, part, part)
        own_rows = rows_of(team.me, index)
        grad = own_sum[rows, :] + reduction.arrived(index)
        standard, inverse = standardize(middle_own[rows, :])
        incoming = cot_all[own_rows, :].astype(FULL)
        grad_mid = incoming + norm_back(grad, gain_row, standard, inverse)
        grad_middle[rows, :] = grad_mid
        branch_low = grad_mid.astype(LOW)
        branch_own[rows, :] = branch_low
        for slot, owner in enumerate((team.sibling, team.far, team.diagonal)):
            side = wo[rows_at(owner * columns, columns, 64), :]
            mixed_out[slot, rows, :] = dot(branch_low, side, NT).astype(LOW)
            exchange(index, slot, owner).start()
        side = wo[rows_at(team.me * columns, columns, 64), :]
        grad_mixed[own_rows, :] = dot(branch_low, side, NT).astype(LOW)
        sums[0:1, :] += column_sums(grad * standard)
        sums[1:2, :] += column_sums(grad)
        sums[2:3, :] += column_sums(branch_low.astype(FULL))
        sums[3:4, :] += column_sums(incoming)
        return nothing

    def exchange(index, slot, owner):
        return team.copy(
            mixed_out.at[slot, rows_at(index * part, part, part)],
            grad_mixed.at[rows_of(team.me, index)],
            a2a_sems.at[2 * index, slot],
            a2a_sems.at[2 * index + 1, slot],
            owner,
        )

    lax.fori_loop(0, own // part, back, 0)
    own_half(0)
    own_rows = rows_at(team.me * own, own, own)
    for source, owner in (
        (mixed_ref.at[own_rows], team.me),
        (pieces.at[0, own_rows], team.sibling),
        (pieces.at[1, own_rows], team.far),
        (pieces.at[2, own_rows], team.diagonal),
    ):
        grad_wo[rows_at(owner * columns, columns, 64), :] = dot(source[...], branch_own[...], TN).astype(LOW)
    down_total.finish(1)
    down_keep.start()
    add_side(0)
    up_keep.start()
    for index in range(own // part):
        for slot, owner in enumerate((team.sibling, team.far, team.diagonal)):
            exchange(index, slot, owner).wait()
    down_keep.wait()
    up_keep.wait()
    for spread in spreads:
        spread.sent()
    for pair in (steps // 2 - 2, steps // 2 - 1):
        slot_copy(pair).wait_send()
    reduction.finish(steps // 2)


def ffn(size, mixed, pieces, x_all, cotangent, wo, up, down, up_bias, out_bias, gain, shift, down_bias):
    length, columns = mixed.shape
    width = x_all.shape[1]
    hidden = up.shape[1]
    own, part = length // 4, 320
    steps = length // part
    pairs = steps // 2

    def shape(dims, kind):
        return jax.ShapeDtypeStruct(dims, kind)

    return pl.pallas_call(
        functools.partial(ffn_kernel, part, size),
        out_shape=(
            shape((own, width), LOW),
            shape((own, width), FULL),
            shape((own, width), FULL),
            shape((length, columns), LOW),
            shape((width // 2, hidden), FULL),
            shape((hidden // 8, width), FULL),
            shape((width, width), LOW),
            shape((8, width), FULL),
        ),
        in_specs=[VMEM] * 12,
        out_specs=(VMEM,) * 4 + (ANY, ANY, VMEM, VMEM),
        scratch_shapes=[
            pltpu.VMEM((own, width), FULL),
            pltpu.VMEM((width // 2, hidden), FULL),
            pltpu.VMEM((hidden // 2, width), FULL),
            pltpu.VMEM((2, width // 2, width), LOW),
            pltpu.VMEM((2, width // 2, width), LOW),
            DMA((2, 2)),
            halving_scratch(size, width // 2, width),
            DMA((2,)),
            pltpu.VMEM((length, width), LOW),
            pltpu.VMEM((length, width), LOW),
            pltpu.VMEM((length, hidden), LOW),
            pltpu.VMEM((length, hidden), LOW),
            pltpu.VMEM((2, part, width), LOW),
            pltpu.VMEM((pairs, part, width), LOW),
            pltpu.VMEM((own, width), FULL),
            pltpu.VMEM((2, part, width), LOW),
            pltpu.VMEM((pairs, part, width), LOW),
            pltpu.VMEM((pairs // 2, part, width), LOW),
            pltpu.VMEM((pairs // 2, part, width), LOW),
            pltpu.VMEM((3, own, columns), LOW),
            pltpu.VMEM((own, width), LOW),
            DMA((own // part, 7)),
            DMA((2, pairs)),
            DMA((4, pairs)),
            DMA((4, 3)),
        ],
        compiler_params=pltpu.CompilerParams(
            collective_id=2, has_side_effects=True, vmem_limit_bytes=63 << 20
        ),
        name="ffn",
    )(mixed, pieces, x_all, cotangent, wo, up, down, up_bias, out_bias, gain, shift, down_bias)


def last_kernel(
    part,
    size,
    dq_ref,
    dk_ref,
    dv_ref,
    wq,
    wk,
    wv,
    normed_all,
    x_all,
    grad_middle,
    gain,
    wo_sum,
    wide,
    input_grad,
    grad_sum,
    vectors,
    own_grad,
    near_out,
    near_in,
    far_out,
    far_in,
    red_sems,
    sources,
    wires,
    total_parts,
    packed,
    packed_in,
    vec_sems,
    keep_sems,
):
    team, plane = Team(), Plane(size)
    length, columns = dq_ref.shape
    width = normed_all.shape[1]
    own = length // 4
    pairs = length // part // 2
    grads = Reduction(team, near_out, near_in, far_out, far_in, red_sems)
    slabs = sources.shape[0]
    lanes_of = width // slabs
    totals = [Direct(plane, sources.at[slab], wires.at[slab], *total_parts[slab]) for slab in range(slabs)]
    others = greet_all(team, plane, True)
    events = Events(totals)

    def slab_grads(slab, nothing):
        lanes = rows_at(slab * lanes_of, lanes_of, lanes_of)
        for index, source in enumerate((dq_ref, dk_ref, dv_ref)):
            value = dot(source[...], normed_all[:, lanes], TN)
            sources[slab, index * columns : (index + 1) * columns, :] = value.astype(LOW)
        sources[slab, 3 * columns : 4 * columns, :] = wo_sum[:, lanes]
        for index, total in enumerate(totals):

            @pl.when(slab == index)
            def _(total=total):
                total.start(0)

        return nothing

    lax.fori_loop(0, slabs, slab_grads, 0)
    gain_row = as_row(gain)
    packed[...] = jnp.zeros_like(packed)
    packed[0:4, :] = wide[0:4, :]
    packed[8:9, :] = wide[4:5, :]
    packed[9:10, 0:columns] = column_sums(dq_ref[...].astype(FULL))
    packed[10:11, 0:columns] = column_sums(dv_ref[...].astype(FULL))

    def step_rows(step):
        return rows_at(owner_at(team.me, step) * own + part_at(step) * part, part, part)

    def compute(step):
        rows = step_rows(step)
        total = dot(dq_ref[rows, :], wq[...], NN) + dot(dk_ref[rows, :], wk[...], NN)
        return total + dot(dv_ref[rows, :], wv[...], NN)

    everything = list(events.waiting)

    def events_at(pair, plan):
        for when, (start, stop) in plan.items():

            @pl.when(pair == when)
            def _(start=start, stop=stop):
                events.waiting = everything[start:stop]
                events.take(1 << 20)

    def pair_step(pair, nothing):
        first, second = 2 * pair, 2 * pair + 1
        grads.give(pair, compute(first))
        standard, unused = standardize(x_all[step_rows(second), :].astype(FULL))
        events_at(pair, {1: (0, 1), 2: (1, 2), 3: (3, 4)})
        values = grads.combine(pair, compute(second))
        packed[4:5, :] += column_sums(values * standard)
        packed[5:6, :] += column_sums(values)

        @pl.when(pair < pairs // 2)
        def _():
            grads.send(pair, values)

        @pl.when(pair >= pairs // 2)
        def _():
            own_grad[rows_at(part_at(second) * part, part, part), :] = values

        events_at(pair, {2: (2, 3), 3: (4, 5)})
        return nothing

    lax.fori_loop(0, pairs, pair_step, 0)
    events.waiting = everything[5:]

    def vector_copy(step):
        return pltpu.make_async_remote_copy(
            src_ref=packed.at[pl.ds(16 * step, 16)],
            dst_ref=packed_in.at[step],
            send_sem=vec_sems.at[0, step],
            recv_sem=vec_sems.at[1, step],
            device_id=others[step],
            device_id_type=MESH,
        )

    def finish_rows(index):
        rows = pl.ds(index * part, part)
        grad = own_grad[rows, :] + grads.arrived(index)
        standard, inverse = standardize(x_all[rows_at(team.me * own + index * part, part, part), :].astype(FULL))
        input_grad[rows, :] = grad_middle[rows, :] + norm_back(grad, gain_row, standard, inverse)

    for step in range(len(others)):
        vector_copy(step).start()
        events.next(1)
        vector_copy(step).wait()
        here = packed[16 * step : 16 * (step + 1), :]
        keep = 16 if step < plane.bits else 8
        row = lax.broadcasted_iota(jnp.int32, here.shape, 0)
        added = here + jnp.where(row < keep, packed_in[step], 0.0)
        packed[16 * (step + 1) : 16 * (step + 2), :] = added
    vectors[...] = packed[16 * len(others) : 16 * (len(others) + 1), :]
    events.take(1 << 20)
    for index in range(own // part):
        finish_rows(index)
    events.end()
    keeps = []
    for slab in range(slabs):
        lanes = pl.ds(slab * lanes_of, lanes_of)
        keeps.append(pltpu.make_async_copy(wires.at[slab], grad_sum.at[:, lanes], keep_sems.at[slab]))
    for keep in keeps:
        keep.start()
    for keep in keeps:
        keep.wait()
    grads.finish(pairs)


def last(size, dq, dk, dv, wq, wk, wv, normed_all, x_all, grad_middle, gain, wo_sum, wide):
    length, columns = dq.shape
    own, width = grad_middle.shape
    part, slabs = 320, 3
    pairs = length // part // 2
    bits = size.bit_length() - 1
    slab = (4 * columns, width // slabs)

    def shape(dims, kind):
        return jax.ShapeDtypeStruct(dims, kind)

    return pl.pallas_call(
        functools.partial(last_kernel, part, size),
        out_shape=(
            shape((own, width), FULL),
            shape((4 * columns, width), LOW),
            shape((16, width), FULL),
        ),
        in_specs=[VMEM] * 12,
        out_specs=(VMEM, ANY, VMEM),
        scratch_shapes=[
            pltpu.VMEM((own, width), FULL),
            pltpu.VMEM((2, part, width), LOW),
            pltpu.VMEM((pairs, part, width), LOW),
            pltpu.VMEM((pairs // 2, part, width), LOW),
            pltpu.VMEM((pairs // 2, part, width), LOW),
            DMA((4, pairs)),
            pltpu.VMEM((slabs, *slab), LOW),
            pltpu.VMEM((slabs, *slab), LOW),
            [direct_scratch(size, *slab) for unused in range(slabs)],
            pltpu.VMEM((16 * (bits + 3), width), FULL),
            pltpu.VMEM((bits + 2, 16, width), FULL),
            DMA((2, bits + 2)),
            DMA((slabs,)),
        ],
        compiler_params=pltpu.CompilerParams(
            collective_id=4, has_side_effects=True, vmem_limit_bytes=60 << 20
        ),
        name="last",
    )(dq, dk, dv, wq, wk, wv, normed_all, x_all, grad_middle, gain, wo_sum, wide)


def local(
    size,
    layer_input,
    segment_ids,
    cotangent,
    attn_gain,
    attn_shift,
    query_weight,
    query_bias,
    key_weight,
    value_weight,
    value_bias,
    out_weight,
    out_bias,
    ffn_gain,
    ffn_shift,
    up_weight,
    up_bias,
    down_weight,
    down_bias,
):
    query_side, key_side, value_side = query_weight.T, key_weight.T, value_weight.T
    x_all, normed_rows, queries, key_rows, value_rows = gather_and_project(
        layer_input,
        attn_gain,
        attn_shift,
        query_side,
        query_bias,
        key_side,
        value_side,
        value_bias,
    )
    mixed, mixed_rot, log_totals, pieces, out_all, q_rot, k_rot, v_rot = attend_forward(
        segment_ids, queries, key_rows, value_rows, out_weight
    )
    out_far, out_own, grad_middle, grad_mixed, up_part, down_part, out_part, sums = ffn(
        size,
        mixed,
        pieces,
        x_all,
        cotangent,
        out_all,
        up_weight,
        down_weight,
        up_bias,
        out_bias,
        ffn_gain,
        ffn_shift,
        down_bias,
    )
    dq, dk, dv, grad_up, grad_down, wo_sum, out_in = attend_backward(
        size, segment_ids, q_rot, k_rot, v_rot, grad_mixed, mixed_rot, log_totals, up_part, down_part, out_part, out_far
    )
    layer_output = (out_own + out_in.astype(FULL)).astype(LOW)
    input_grad, grads, vectors = last(
        size,
        dq,
        dk,
        dv,
        query_side,
        key_side,
        value_side,
        normed_rows,
        x_all,
        grad_middle,
        attn_gain,
        wo_sum,
        sums,
    )
    columns = query_side.shape[0]
    grads = grads.astype(FULL)
    return (
        layer_output,
        input_grad,
        vectors[4],
        vectors[5],
        grads[0:columns].T,
        vectors[9, 0:columns],
        grads[columns : 2 * columns].T,
        grads[2 * columns : 3 * columns].T,
        vectors[10, 0:columns],
        grads[3 * columns :],
        vectors[2],
        vectors[0],
        vectors[1],
        grad_up.astype(FULL),
        vectors[8],
        grad_down.astype(FULL),
        vectors[3],
    )


def solution(mesh):
    return jax.shard_map(
        functools.partial(local, mesh.shape["dp"]),
        mesh=mesh,
        in_specs=(
            P(("dp", "seq"), None),
            P("dp", None),
            P(("dp", "seq"), None),
            P(),
            P(),
            P(None, "seq"),
            P("seq"),
            P(None, "seq"),
            P(None, "seq"),
            P("seq"),
            P("seq", None),
            P(),
            P(),
            P(),
            P(None, "seq"),
            P("seq"),
            P("seq", None),
            P(),
        ),
        out_specs=(
            P(("dp", "seq"), None),
            P(("dp", "seq"), None),
            P(),
            P(),
            P(None, "seq"),
            P("seq"),
            P(None, "seq"),
            P(None, "seq"),
            P("seq"),
            P("seq", None),
            P(),
            P(),
            P(),
            P(None, "seq"),
            P("seq"),
            P("seq", None),
            P(),
        ),
        check_vma=False,
    )
```

profile of v0, /device:TPU:0, one launch (start us, length us, event | category | flops | bytes accessed | tf_op | source)
XLA Modules:
  0.0 297.0 jit_solution(15610737650049411077)
XLA Ops:
  0.7 0.0 copy-start.3
  0.7 1.0 copy-done.3
  1.6 1.0 copy-done.4
  2.6 1.0 copy-done.5
  3.5 1.2 copy-done.6
  4.7 0.7 copy-done.7
  5.4 0.7 copy-done.8
  6.1 0.7 copy-done.9
  6.8 0.7 copy-done.10
  7.4 30.0 %gather_and_project.1 = (bf16[2560,768]{1,0:T(8,128)(2,1)}, bf16[2560,768]{1,0:T(8,128)(2,1)}, bf16[2560,192]{1,0:T(8,128)(2,1)S(1)}, bf16[2560,192]{1,0:T(8,128)(2,1)S(1)}, bf16[2560,192]{1,0:T(8,128)(2,1)S(1)}) custom-call(bf16[640,768]{1,0:T(8,128)(2,1)S(1)} %copy-done.6, bf16[768]{0:T(1024)(128)(2,1)S(1)} %copy-done.7, bf16[768]{0:T(1024)(128)(2,1)S(1)} %copy-done.8, ...), custom_call_target="tpu_custom_call" | custom-call | tf_op jit(solution)/shard_map/gather_and_project/pallas_call | solution.py:945
  37.4 0.0 copy-start
  37.4 1.0 copy-done
  38.5 1.1 copy-done.1
  39.5 1.1 copy-done.2
  40.6 46.6 %attend_forward.1 = (bf16[2560,192]{1,0:T(8,128)(2,1)}, f32[392,8,192]{2,1,0:T(8,128)}, f32[2560,128]{1,0:T(8,128)}, bf16[3,2560,192]{2,1,0:T(8,128)(2,1)}, bf16...) custom-call(s32[1,2560]{1,0:T(1,128)} %spans.3, ...), custom_call_target="tpu_custom_call" | custom-call | tf_op jit(solution)/shard_map/attend_forward/pallas_call | solution.py:340
  87.2 76.7 %ffn.1 = (bf16[640,768]{1,0:T(8,128)(2,1)}, f32[640,768]{1,0:T(8,128)}, f32[640,768]{1,0:T(8,128)}, bf16[2560,192]{1,0:T(8,128)(2,1)}, f32[384,768]{1,0:T(8,128)...) custom-call(bf16[2560,192]{1,0:T(8,128)(2,1)} %get-tuple-element.51.mixed_ref, ...), custom_call_target="tpu_custom_call" | custom-call | tf_op jit(solution)/shard_map/ffn/pallas_call | solution.py:1357
  163.9 63.2 %attend_backward.1 = (bf16[2560,192]{1,0:T(8,128)(2,1)}, bf16[2560,192]{1,0:T(8,128)(2,1)}, bf16[2560,192]{1,0:T(8,128)(2,1)}, bf16[768,768]{1,0:T(8,128)(2,1)},...) custom-call(s32[1,2560]{1,0:T(1,128)} %spans.3, ...), custom_call_target="tpu_custom_call" | custom-call | tf_op jit(solution)/shard_map/attend_backward/pallas_call | solution.py:807
  227.0 0.0 copy-start.13
  227.0 57.4 %last.1 = (f32[640,768]{1,0:T(8,128)}, bf16[768,768]{1,0:T(8,128)(2,1)}, f32[16,768]{1,0:T(8,128)}) custom-call(bf16[2560,192]{1,0:T(8,128)(2,1)} %get-tuple-element.67.dq_ref, bf16[2560,192]{1,0:T(8,128)(2,1)} %get-tuple-element.68.dk_ref, bf16[2560,192]{1,0:T(8,128)(2,1)} %get-tuple-element.69.dv_ref, bf16[192,768]{1,0:T(8,128)(2,1)} %bitcast.11, ...), custom_call_target="tpu_custom_call" | custom-call | tf_op jit(solution)/shard_map/last/pallas_call | solution.py:1564
  284.5 1.1 add_convert_fusion
  285.7 1.3 fusion
  287.0 1.8 slice_reduce_fusion
  288.8 0.9 slice.55
  289.6 0.2 convert_element_type.17
  289.8 0.0 copy-start.15
  289.8 1.2 slice_bitcast_fusion
  291.0 0.7 copy-done.15
  291.7 1.6 convert_element_type.18
  293.3 0.1 copy-done.14
  293.4 1.6 convert_element_type.19
  294.9 0.8 copy-done.12
  295.8 1.3 copy.36
  (16 shorter events, 0.0 us)
Async XLA Ops:
  0.7 1.0 copy-start.3
  1.6 1.0 copy-start.4
  2.6 1.0 copy-start.5
  3.5 1.2 copy-start.6
  4.7 0.7 copy-start.7
  5.4 0.7 copy-start.8
  6.1 0.7 copy-start.9
  6.8 0.7 copy-start.10
  37.4 1.1 copy-start
  38.5 1.1 copy-start.1
  39.5 1.1 copy-start.2
  227.0 57.5 %copy-start.13 = (f32[640,768]{1,0:T(8,128)S(1)}, f32[640,768]{1,0:T(8,128)}, u32[]{:S(2)}) copy-start(f32[640,768]{1,0:T(8,128)} %get-tuple-element.55) | copy-start | bytes 5898244
  227.0 57.5 %copy-start.16 = (bf16[640,768]{1,0:T(8,128)(2,1)S(1)}, bf16[640,768]{1,0:T(8,128)(2,1)}, u32[]{:S(2)}) copy-start(bf16[640,768]{1,0:T(8,128)(2,1)} %get-tuple-element.66) | copy-start | bytes 2949124
  284.5 4.3 %copy-start.11 = (bf16[768,768]{1,0:T(8,128)(2,1)S(1)}, bf16[768,768]{1,0:T(8,128)(2,1)}, u32[]{:S(2)}) copy-start(bf16[768,768]{1,0:T(8,128)(2,1)} %get-tuple-element.76) | copy-start | bytes 3538948
  289.8 1.9 copy-start.15
  291.7 1.7 copy-start.14
  293.4 2.4 copy-start.12
where the time goes:
time: 298 us; the launch traced here: 297 us
  Pallas kernels  274 us (92%)
  local copies, waits for them, and re-layouts  18 us (6%)
  other arithmetic  4.46 us (1%)
    pallas_call x1, Pallas kernels, ffn(): pl.pallas_call(functools.partial(ffn_kernel, part, size), out_shape=(shap...  76.7 us
    pallas_call x1, Pallas kernels, attend_backward(): pl.pallas_call(functools.partial(backward_kernel, 256, 512, head_count, s...  63.2 us
    pallas_call x1, Pallas kernels, last(): pl.pallas_call(functools.partial(last_kernel, part, size), out_shape=(sha...  57.4 us
    pallas_call x1, Pallas kernels, attend_forward(): pl.pallas_call(functools.partial(forward_kernel, 256, 512, head_count), o...  46.6 us
    pallas_call x1, Pallas kernels, gather_and_project(): pl.pallas_call(functools.partial(project_kernel, part), out_shape=(wide,...  30 us
    unnamed x35, local copies, waits for them, and re-layouts  12.8 us

commit v1 on v0

--- a/solution.py
+++ b/solution.py
@@ -56,6 +56,10 @@
             device_id=self.device(other),
             device_id_type=MESH,
         )
+
+
+def loads_of(pairs, sems):
+    return [pltpu.make_async_copy(source, target, sems.at[index]) for index, (source, target) in enumerate(pairs)]
 
 
 def rows_at(start, count, multiple):
@@ -609,12 +613,12 @@
     head_count,
     size,
     spans,
-    q_rot,
-    k_rot,
-    v_rot,
-    d_ref,
-    mixed_rot_ref,
-    log_ref,
+    q_hbm,
+    k_hbm,
+    v_hbm,
+    d_hbm,
+    mixed_hbm,
+    log_hbm,
     up_part,
     down_part,
     wo_part,
@@ -646,6 +650,13 @@
     out_sems,
     keep_sems,
     dq_side,
+    q_rot,
+    k_rot,
+    v_rot,
+    d_ref,
+    mixed_rot_ref,
+    log_ref,
+    load_sems,
 ):
     length, width = q_rot.shape
     small = length - LONGEST
@@ -668,6 +679,17 @@
     for load in loads:
         load.wait()
     events.start()
+    arrays = (
+        (q_hbm, q_rot),
+        (k_hbm, k_rot),
+        (v_hbm, v_rot),
+        (d_hbm, d_ref),
+        (mixed_hbm, mixed_rot_ref),
+        (log_hbm, log_ref),
+    )
+    fetches = loads_of(arrays, load_sems)
+    for fetch in fetches:
+        fetch.start()
     out_copy = team.copy(out_far, out_in, out_sems.at[0], out_sems.at[1], team.far)
     out_copy.start()
 
@@ -682,6 +704,8 @@
         copy.start()
     wo_across = team.copy(wo_far.at[0], wo_far.at[1], wo_sems.at[0, 2], wo_sems.at[1, 2], team.far)
 
+    for fetch in fetches:
+        fetch.wait()
     rotate_into(d_ref, d_rot, dq_turned, offset)
     q_all, k_all, d_all = q_rot[...], k_rot[...], d_rot[...]
     q_turned[...] = jnp.transpose(q_all)
@@ -808,7 +832,7 @@
         functools.partial(backward_kernel, 256, 512, head_count, size),
         out_shape=(shape((length, width)),) * 3
         + (shape(whole), shape(whole), shape(wo_shape), shape(out_far.shape)),
-        in_specs=[SMEM] + [VMEM] * 6 + [ANY, ANY, VMEM, ANY],
+        in_specs=[SMEM] + [ANY] * 8 + [VMEM, ANY],
         out_specs=(VMEM,) * 3 + (ANY, ANY, VMEM, ANY),
         scratch_shapes=[
             pltpu.VMEM((length, width), low),
@@ -831,6 +855,13 @@
             DMA((2,)),
             DMA((4,)),
             pltpu.VMEM((width, length), full),
+            pltpu.VMEM((length, width), low),
+            pltpu.VMEM((length, width), low),
+            pltpu.VMEM((length, width), low),
+            pltpu.VMEM((length, width), low),
+            pltpu.VMEM(mixed_rot.shape, full),
+            pltpu.VMEM(log_totals.shape, full),
+            DMA((6,)),
         ],
         compiler_params=pltpu.CompilerParams(
             collective_id=3, has_side_effects=True, vmem_limit_bytes=63 << 20
@@ -958,7 +989,7 @@
             DMA((4,)),
         ],
         compiler_params=pltpu.CompilerParams(
-            collective_id=0, has_side_effects=True, vmem_limit_bytes=48 << 20
+            collective_id=0, has_side_effects=True, vmem_limit_bytes=63 << 20
         ),
         name="gather_and_project",
     )(x, gain, shift, wq, bq, wk, wv, bv)
@@ -1026,13 +1057,13 @@
 def ffn_kernel(
     part,
     size,
-    mixed_ref,
-    pieces,
-    x_all,
+    mixed_hbm,
+    pieces_hbm,
+    x_hbm,
     cot_ref,
-    wo,
-    up,
-    down,
+    wo_hbm,
+    up_hbm,
+    down_hbm,
     up_bias,
     out_bias,
     gain,
@@ -1071,6 +1102,13 @@
     slot_sems,
     red_sems,
     a2a_sems,
+    mixed_ref,
+    pieces,
+    x_all,
+    wo,
+    up,
+    down,
+    load_sems,
 ):
     team = Team()
     length = mixed_ref.shape[0]
@@ -1108,6 +1146,12 @@
 
     for spread in spreads:
         spread.start()
+    arrays = (mixed_hbm, mixed_ref), (pieces_hbm, pieces), (x_hbm, x_all), (wo_hbm, wo), (up_hbm, up), (down_hbm, down)
+    loads = loads_of(arrays, load_sems)
+    for load in loads:
+        load.start()
+    for load in loads:
+        load.wait()
     sums[...] = jnp.zeros_like(sums)
     gain_row, shift_row, bias_row = as_row(gain), as_row(shift), as_row(out_bias)
     up_row, down_row = as_row(up_bias), as_row(down_bias)
@@ -1366,7 +1410,7 @@
             shape((width, width), LOW),
             shape((8, width), FULL),
         ),
-        in_specs=[VMEM] * 12,
+        in_specs=[ANY] * 7 + [VMEM] * 5,
         out_specs=(VMEM,) * 4 + (ANY, ANY, VMEM, VMEM),
         scratch_shapes=[
             pltpu.VMEM((own, width), FULL),
@@ -1394,6 +1438,13 @@
             DMA((2, pairs)),
             DMA((4, pairs)),
             DMA((4, 3)),
+            pltpu.VMEM(mixed.shape, LOW),
+            pltpu.VMEM(pieces.shape, LOW),
+            pltpu.VMEM(x_all.shape, LOW),
+            pltpu.VMEM(wo.shape, LOW),
+            pltpu.VMEM(up.shape, LOW),
+            pltpu.VMEM(down.shape, LOW),
+            DMA((6,)),
         ],
         compiler_params=pltpu.CompilerParams(
             collective_id=2, has_side_effects=True, vmem_limit_bytes=63 << 20
@@ -1405,15 +1456,15 @@
 def last_kernel(
     part,
     size,
-    dq_ref,
-    dk_ref,
-    dv_ref,
+    dq_hbm,
+    dk_hbm,
+    dv_hbm,
     wq,
     wk,
     wv,
-    normed_all,
-    x_all,
-    grad_middle,
+    normed_hbm,
+    x_hbm,
+    grad_hbm,
     gain,
     wo_sum,
     wide,
@@ -1433,8 +1484,26 @@
     packed_in,
     vec_sems,
     keep_sems,
+    dq_ref,
+    dk_ref,
+    dv_ref,
+    normed_all,
+    x_all,
+    grad_middle,
+    load_sems,
 ):
     team, plane = Team(), Plane(size)
+    arrays = (
+        (dq_hbm, dq_ref),
+        (dk_hbm, dk_ref),
+        (dv_hbm, dv_ref),
+        (normed_hbm, normed_all),
+        (x_hbm, x_all),
+        (grad_hbm, grad_middle),
+    )
+    loads = loads_of(arrays, load_sems)
+    for load in loads:
+        load.start()
     length, columns = dq_ref.shape
     width = normed_all.shape[1]
     own = length // 4
@@ -1460,7 +1529,11 @@
 
         return nothing
 
+    for load in loads[:4]:
+        load.wait()
     lax.fori_loop(0, slabs, slab_grads, 0)
+    for load in loads[4:]:
+        load.wait()
     gain_row = as_row(gain)
     packed[...] = jnp.zeros_like(packed)
     packed[0:4, :] = wide[0:4, :]
@@ -1568,7 +1641,7 @@
             shape((4 * columns, width), LOW),
             shape((16, width), FULL),
         ),
-        in_specs=[VMEM] * 12,
+        in_specs=[ANY] * 3 + [VMEM] * 3 + [ANY] * 3 + [VMEM] * 3,
         out_specs=(VMEM, ANY, VMEM),
         scratch_shapes=[
             pltpu.VMEM((own, width), FULL),
@@ -1584,6 +1657,13 @@
             pltpu.VMEM((bits + 2, 16, width), FULL),
             DMA((2, bits + 2)),
             DMA((slabs,)),
+            pltpu.VMEM(dq.shape, LOW),
+            pltpu.VMEM(dk.shape, LOW),
+            pltpu.VMEM(dv.shape, LOW),
+            pltpu.VMEM(normed_all.shape, LOW),
+            pltpu.VMEM(x_all.shape, LOW),
+            pltpu.VMEM(grad_middle.shape, FULL),
+            DMA((6,)),
         ],
         compiler_params=pltpu.CompilerParams(
             collective_id=4, has_side_effects=True, vmem_limit_bytes=60 << 20

time: 298 us -> 285 us (0.956)
  local copies, waits for them, and re-layouts: 18 us -> 8.03 us
  Pallas kernels: 274 us -> 271 us
    unnamed x35 -> x13, local copies, waits for them, and re-layouts: 12.8 us -> 2.86 us
    pallas_call x1, Pallas kernels: 57.4 us -> 54 us  [last(): pl.pallas_call(functools.partial(last_kernel, part, size), out_shape=(sha...]
where the time goes in v1:
time: 285 us; the launch traced here: 284 us
  Pallas kernels  271 us (95%)
  local copies, waits for them, and re-layouts  8.03 us (3%)
  other arithmetic  4.46 us (2%)
    pallas_call x1, Pallas kernels, ffn(): pl.pallas_call(functools.partial(ffn_kernel, part, size), out_shape=(shap...  76.7 us
    pallas_call x1, Pallas kernels, attend_backward(): pl.pallas_call(functools.partial(backward_kernel, 256, 512, head_count, s...  60.9 us
    pallas_call x1, Pallas kernels, last(): pl.pallas_call(functools.partial(last_kernel, part, size), out_shape=(sha...  54 us
    pallas_call x1, Pallas kernels, attend_forward(): pl.pallas_call(functools.partial(forward_kernel, 256, 512, head_count), o...  46.4 us
    pallas_call x1, Pallas kernels, gather_and_project(): pl.pallas_call(functools.partial(project_kernel, part), out_shape=(wide,...  32.8 us

profile of v1, /device:TPU:0, one launch (start us, length us, event | category | flops | bytes accessed | tf_op | source)
XLA Modules:
  0.0 284.2 jit_solution(16333581429526170406)
XLA Ops:
  0.7 32.8 %gather_and_project.1 = (bf16[2560,768]{1,0:T(8,128)(2,1)}, bf16[2560,768]{1,0:T(8,128)(2,1)}, bf16[2560,192]{1,0:T(8,128)(2,1)}, bf16[2560,192]{1,0:T(8,128)(2,1)}, bf16[2560,192]{1,0:T(8,128)(2,1)}) custom-call(bf16[640,768]{1,0:T(8,128)(2,1)} %x_ref.1, bf16[768]{0:T(1024)(128)(2,1)} %gain.5, bf16[768]{0:T(1024)(128)(2,1)} %shift.2, ...), custom_call_target="tpu_custom_call" | custom-call | tf_op jit(solution)/shard_map/gather_and_project/pallas_call | solution.py:976
  33.5 46.4 %attend_forward.1 = (bf16[2560,192]{1,0:T(8,128)(2,1)}, f32[392,8,192]{2,1,0:T(8,128)}, f32[2560,128]{1,0:T(8,128)}, bf16[3,2560,192]{2,1,0:T(8,128)(2,1)}, bf16...) custom-call(s32[1,2560]{1,0:T(1,128)} %spans.3, ...), custom_call_target="tpu_custom_call" | custom-call | tf_op jit(solution)/shard_map/attend_forward/pallas_call | solution.py:344
  79.9 76.7 %ffn.1 = (bf16[640,768]{1,0:T(8,128)(2,1)}, f32[640,768]{1,0:T(8,128)}, f32[640,768]{1,0:T(8,128)}, bf16[2560,192]{1,0:T(8,128)(2,1)}, f32[384,768]{1,0:T(8,128)...) custom-call(bf16[2560,192]{1,0:T(8,128)(2,1)} %get-tuple-element.51.mixed_hbm, ...), custom_call_target="tpu_custom_call" | custom-call | tf_op jit(solution)/shard_map/ffn/pallas_call | solution.py:1401
  156.7 60.9 %attend_backward.1 = (bf16[2560,192]{1,0:T(8,128)(2,1)}, bf16[2560,192]{1,0:T(8,128)(2,1)}, bf16[2560,192]{1,0:T(8,128)(2,1)}, bf16[768,768]{1,0:T(8,128)(2,1)},...) custom-call(s32[1,2560]{1,0:T(1,128)} %spans.3, ...), custom_call_target="tpu_custom_call" | custom-call | tf_op jit(solution)/shard_map/attend_backward/pallas_call | solution.py:831
  217.6 0.0 copy-start.2
  217.6 0.0 copy-start.5
  217.6 54.0 %last.1 = (f32[640,768]{1,0:T(8,128)}, bf16[768,768]{1,0:T(8,128)(2,1)}, f32[16,768]{1,0:T(8,128)}) custom-call(bf16[2560,192]{1,0:T(8,128)(2,1)} %get-tuple-element.67.dq_hbm, bf16[2560,192]{1,0:T(8,128)(2,1)} %get-tuple-element.68.dk_hbm, bf16[2560,192]{1,0:T(8,128)(2,1)} %get-tuple-element.69.dv_hbm, bf16[192,768]{1,0:T(8,128)(2,1)} %bitcast.12, ...), custom_call_target="tpu_custom_call" | custom-call | tf_op jit(solution)/shard_map/last/pallas_call | solution.py:1637
  271.7 0.0 copy-done.2
  271.7 0.0 copy-done.5
  271.7 0.0 copy-start
  271.7 1.1 add_convert_fusion
  272.8 1.3 fusion
  274.2 1.7 slice_reduce_fusion
  275.9 0.0 copy-done
  275.9 0.9 slice.55
  276.8 0.2 convert_element_type.17
  277.0 0.0 copy-start.4
  277.0 1.2 slice_bitcast_fusion
  278.2 0.7 copy-done.4
  278.9 0.0 copy-start.3
  278.9 1.6 convert_element_type.18
  280.4 0.1 copy-done.3
  280.5 0.0 copy-start.1
  280.5 1.6 convert_element_type.19
  282.1 0.8 copy-done.1
  282.9 1.3 copy.36
Async XLA Ops:
  217.6 54.1 %copy-start.2 = (f32[640,768]{1,0:T(8,128)S(1)}, f32[640,768]{1,0:T(8,128)}, u32[]{:S(2)}) copy-start(f32[640,768]{1,0:T(8,128)} %get-tuple-element.55) | copy-start | bytes 5898244
  217.6 54.1 %copy-start.5 = (bf16[640,768]{1,0:T(8,128)(2,1)S(1)}, bf16[640,768]{1,0:T(8,128)(2,1)}, u32[]{:S(2)}) copy-start(bf16[640,768]{1,0:T(8,128)(2,1)} %get-tuple-element.66) | copy-start | bytes 2949124
  271.7 4.2 %copy-start = (bf16[768,768]{1,0:T(8,128)(2,1)S(1)}, bf16[768,768]{1,0:T(8,128)(2,1)}, u32[]{:S(2)}) copy-start(bf16[768,768]{1,0:T(8,128)(2,1)} %get-tuple-element.76) | copy-start | bytes 3538948
  277.0 1.9 copy-start.4
  278.9 1.7 copy-start.3
  280.5 2.4 copy-start.1

commit v2 on v1

--- a/solution.py
+++ b/solution.py
@@ -210,15 +210,19 @@
     log_ref,
     pieces,
     wo_all,
-    q_rot,
-    k_rot,
-    v_rot,
+    q_hbm,
+    k_hbm,
+    v_hbm,
     v_heads,
     buffer,
     wo_sems,
     far_sems,
     near_sems,
     pass_sems,
+    q_rot,
+    k_rot,
+    v_rot,
+    store_sems,
 ):
     length, width = q_ref.shape
     team = Team()
@@ -250,6 +254,7 @@
     rotate_into(q_ref, q_rot, buffer, offset)
     rotate_into(k_ref, k_rot, buffer, offset)
     rotate_into(v_ref, v_rot, buffer, offset)
+    stores = loads_of(((q_rot, q_hbm), (k_rot, k_hbm), (v_rot, v_hbm)), store_sems)
     v_all = v_rot[...]
     for head in range(head_count):
         v_heads[head] = jnp.concatenate(
@@ -301,6 +306,8 @@
         return nothing
 
     lax.fori_loop(0, small // rows_of, little, 0)
+    for store in stores:
+        store.start()
     lag, trips = 2, LONGEST // rows_of
 
     def large(index, nothing):
@@ -336,6 +343,8 @@
     spread.near().wait_recv()
     spread.passed().wait_recv()
     spread.kept().wait()
+    for store in stores:
+        store.wait()
 
 
 def attend_forward(spans, queries, key_rows, value_rows, out_weight):
@@ -354,7 +363,7 @@
             jax.ShapeDtypeStruct((length, width), LOW),
         ),
         in_specs=[SMEM, VMEM, VMEM, VMEM, VMEM],
-        out_specs=(VMEM, VMEM, VMEM, ANY, ANY, VMEM, VMEM, VMEM),
+        out_specs=(VMEM, VMEM, VMEM, ANY, ANY, ANY, ANY, ANY),
         scratch_shapes=[
             pltpu.VMEM((head_count, length, 256), jnp.bfloat16),
             pltpu.VMEM((length // 8 + EXTRA, 8, width), FULL),
@@ -362,6 +371,10 @@
             DMA((2, length // 256)),
             DMA((2, length // 256)),
             DMA((2, length // 256)),
+            pltpu.VMEM((length, width), LOW),
+            pltpu.VMEM((length, width), LOW),
+            pltpu.VMEM((length, width), LOW),
+            DMA((3,)),
         ],
         compiler_params=pltpu.CompilerParams(
             collective_id=1, has_side_effects=True, vmem_limit_bytes=60 << 20
@@ -761,8 +774,8 @@
         def before(head):
             for trip in range(trips):
                 slot = trip * head_count + head
-                limit = (slot + 1) // 2
-                earlier = slot // 2
+                limit = (slot * 2 + 3) // 5
+                earlier = (slot * 2 + 1) // 5
                 if limit > earlier:
 
                     @pl.when(index == trip)
@@ -1563,7 +1576,7 @@
         first, second = 2 * pair, 2 * pair + 1
         grads.give(pair, compute(first))
         standard, unused = standardize(x_all[step_rows(second), :].astype(FULL))
-        events_at(pair, {1: (0, 1), 2: (1, 2), 3: (3, 4)})
+        events_at(pair, {1: (0, 1), 2: (1, 2), 3: (2, 4)})
         values = grads.combine(pair, compute(second))
         packed[4:5, :] += column_sums(values * standard)
         packed[5:6, :] += column_sums(values)
@@ -1576,7 +1589,7 @@
         def _():
             own_grad[rows_at(part_at(second) * part, part, part), :] = values
 
-        events_at(pair, {2: (2, 3), 3: (4, 5)})
+        events_at(pair, {3: (4, 5)})
         return nothing
 
     lax.fori_loop(0, pairs, pair_step, 0)

time: 285 us -> 282 us (0.989)
  no operation moved by 1% of the time
where the time goes in v2:
time: 282 us
  Pallas kernels  269 us (95%)
  local copies, waits for them, and re-layouts  8.03 us (3%)
  other arithmetic  4.46 us (2%)
    pallas_call x1, Pallas kernels, ffn(): pl.pallas_call(functools.partial(ffn_kernel, part, size), out_shape=(shap...  76.7 us
    pallas_call x1, Pallas kernels, attend_backward(): pl.pallas_call(functools.partial(backward_kernel, 256, 512, head_count, s...  60.7 us
    pallas_call x1, Pallas kernels, last(): pl.pallas_call(functools.partial(last_kernel, part, size), out_shape=(sha...  52.9 us
    pallas_call x1, Pallas kernels, attend_forward(): pl.pallas_call(functools.partial(forward_kernel, 256, 512, head_count), o...  45.4 us
    pallas_call x1, Pallas kernels, gather_and_project(): pl.pallas_call(functools.partial(project_kernel, part), out_shape=(wide,...  32.8 us

profile of v2, /device:TPU:0, one launch (start us, length us, event | category | flops | bytes accessed | tf_op | source)
XLA Modules:
  0.0 281.8 jit_solution(4945546492245480475)
XLA Ops:
  0.7 32.8 %gather_and_project.1 = (bf16[2560,768]{1,0:T(8,128)(2,1)}, bf16[2560,768]{1,0:T(8,128)(2,1)}, bf16[2560,192]{1,0:T(8,128)(2,1)}, bf16[2560,192]{1,0:T(8,128)(2,1)}, bf16[2560,192]{1,0:T(8,128)(2,1)}) custom-call(bf16[640,768]{1,0:T(8,128)(2,1)} %x_ref.1, bf16[768]{0:T(1024)(128)(2,1)} %gain.5, bf16[768]{0:T(1024)(128)(2,1)} %shift.2, ...), custom_call_target="tpu_custom_call" | custom-call | tf_op jit(solution)/shard_map/gather_and_project/pallas_call | solution.py:989
  33.5 45.4 %attend_forward.1 = (bf16[2560,192]{1,0:T(8,128)(2,1)}, f32[392,8,192]{2,1,0:T(8,128)}, f32[2560,128]{1,0:T(8,128)}, bf16[3,2560,192]{2,1,0:T(8,128)(2,1)}, bf16...) custom-call(s32[1,2560]{1,0:T(1,128)} %spans.3, ...), custom_call_target="tpu_custom_call" | custom-call | tf_op jit(solution)/shard_map/attend_forward/pallas_call | solution.py:353
  78.9 76.7 %ffn.1 = (bf16[640,768]{1,0:T(8,128)(2,1)}, f32[640,768]{1,0:T(8,128)}, f32[640,768]{1,0:T(8,128)}, bf16[2560,192]{1,0:T(8,128)(2,1)}, f32[384,768]{1,0:T(8,128)...) custom-call(bf16[2560,192]{1,0:T(8,128)(2,1)} %get-tuple-element.51.mixed_hbm, ...), custom_call_target="tpu_custom_call" | custom-call | tf_op jit(solution)/shard_map/ffn/pallas_call | solution.py:1414
  155.6 60.7 %attend_backward.1 = (bf16[2560,192]{1,0:T(8,128)(2,1)}, bf16[2560,192]{1,0:T(8,128)(2,1)}, bf16[2560,192]{1,0:T(8,128)(2,1)}, bf16[768,768]{1,0:T(8,128)(2,1)},...) custom-call(s32[1,2560]{1,0:T(1,128)} %spans.3, ...), custom_call_target="tpu_custom_call" | custom-call | tf_op jit(solution)/shard_map/attend_backward/pallas_call | solution.py:844
  216.3 0.0 copy-start.2
  216.3 0.0 copy-start.5
  216.3 52.9 %last.1 = (f32[640,768]{1,0:T(8,128)}, bf16[768,768]{1,0:T(8,128)(2,1)}, f32[16,768]{1,0:T(8,128)}) custom-call(bf16[2560,192]{1,0:T(8,128)(2,1)} %get-tuple-element.67.dq_hbm, bf16[2560,192]{1,0:T(8,128)(2,1)} %get-tuple-element.68.dk_hbm, bf16[2560,192]{1,0:T(8,128)(2,1)} %get-tuple-element.69.dv_hbm, bf16[192,768]{1,0:T(8,128)(2,1)} %bitcast.12, ...), custom_call_target="tpu_custom_call" | custom-call | tf_op jit(solution)/shard_map/last/pallas_call | solution.py:1650
  269.2 0.0 copy-done.2
  269.2 0.0 copy-done.5
  269.2 0.0 copy-start
  269.2 1.1 add_convert_fusion
  270.4 1.3 fusion
  271.7 1.7 slice_reduce_fusion
  273.5 0.0 copy-done
  273.5 0.9 slice.55
  274.3 0.2 convert_element_type.17
  274.5 0.0 copy-start.4
  274.5 1.2 slice_bitcast_fusion
  275.8 0.7 copy-done.4
  276.4 0.0 copy-start.3
  276.4 1.6 convert_element_type.18
  278.0 0.1 copy-done.3
  278.1 0.0 copy-start.1
  278.1 1.6 convert_element_type.19
  279.7 0.8 copy-done.1
  280.5 1.3 copy.36
Async XLA Ops:
  216.3 52.9 %copy-start.2 = (f32[640,768]{1,0:T(8,128)S(1)}, f32[640,768]{1,0:T(8,128)}, u32[]{:S(2)}) copy-start(f32[640,768]{1,0:T(8,128)} %get-tuple-element.55) | copy-start | bytes 5898244
  216.3 52.9 %copy-start.5 = (bf16[640,768]{1,0:T(8,128)(2,1)S(1)}, bf16[640,768]{1,0:T(8,128)(2,1)}, u32[]{:S(2)}) copy-start(bf16[640,768]{1,0:T(8,128)(2,1)} %get-tuple-element.66) | copy-start | bytes 2949124
  269.2 4.2 %copy-start = (bf16[768,768]{1,0:T(8,128)(2,1)S(1)}, bf16[768,768]{1,0:T(8,128)(2,1)}, u32[]{:S(2)}) copy-start(bf16[768,768]{1,0:T(8,128)(2,1)} %get-tuple-element.76) | copy-start | bytes 3538948
  274.5 1.9 copy-start.4
  276.4 1.7 copy-start.3
  278.1 2.4 copy-start.1

commit v3 on v2

--- a/solution.py
+++ b/solution.py
@@ -894,10 +894,10 @@
     wv,
     bv,
     x_all,
-    normed,
-    q_ref,
-    k_ref,
-    v_ref,
+    normed_hbm,
+    q_hbm,
+    k_hbm,
+    v_hbm,
     landing,
     far_send,
     far_recv,
@@ -906,6 +906,11 @@
     pass_send,
     pass_recv,
     keep_sem,
+    normed,
+    q_ref,
+    k_ref,
+    v_ref,
+    store_sems,
 ):
     team = Team()
     own = x_ref.shape[0]
@@ -952,7 +957,14 @@
         project(team.me, index, x_ref[rows_at(index * part, part, part), :])
         return nothing
 
+    def stores(slot, owner):
+        rows = rows_at(owner * own, own, own)
+        arrays = (normed, normed_hbm), (q_ref, q_hbm), (k_ref, k_hbm), (v_ref, v_hbm)
+        return loads_of([(source.at[rows], target.at[rows]) for source, target in arrays], store_sems.at[slot])
+
     lax.fori_loop(0, count, mine, 0)
+    for store in stores(0, team.me):
+        store.start()
     near.wait()
 
     def next_to(index, nothing):
@@ -960,6 +972,8 @@
         return nothing
 
     lax.fori_loop(0, count, next_to, 0)
+    for store in stores(1, team.sibling):
+        store.start()
 
     def across(index, nothing):
         far_copy(index).wait_recv()
@@ -970,11 +984,17 @@
         return nothing
 
     lax.fori_loop(0, count, across, 0)
+    for slot, owner in ((2, team.far), (3, team.diagonal)):
+        for store in stores(slot, owner):
+            store.start()
     for slot, owner in ((1, team.sibling), (2, team.far), (3, team.diagonal)):
         keep(owner, landing.at[rows_at(owner * own, own, own)], slot).start()
     for slot, owner in ((1, team.sibling), (2, team.far), (3, team.diagonal)):
         keep(owner, landing.at[rows_at(owner * own, own, own)], slot).wait()
     keep(team.me, x_ref, 0).wait()
+    for slot, owner in enumerate((team.me, team.sibling, team.far, team.diagonal)):
+        for store in stores(slot, owner):
+            store.wait()
     for index in range(count):
         far_copy(index).wait_send()
         pass_copy(index).wait_send()
@@ -990,7 +1010,7 @@
         functools.partial(project_kernel, part),
         out_shape=(wide, wide, narrow, narrow, narrow),
         in_specs=[VMEM] * 8,
-        out_specs=(ANY, VMEM, VMEM, VMEM, VMEM),
+        out_specs=(ANY,) * 5,
         scratch_shapes=[
             pltpu.VMEM((length, width), LOW),
             DMA((count,)),
@@ -1000,6 +1020,11 @@
             DMA((count,)),
             DMA((count,)),
             DMA((4,)),
+            pltpu.VMEM((length, width), LOW),
+            pltpu.VMEM((length, columns), LOW),
+            pltpu.VMEM((length, columns), LOW),
+            pltpu.VMEM((length, columns), LOW),
+            DMA((4, 4)),
         ],
         compiler_params=pltpu.CompilerParams(
             collective_id=0, has_side_effects=True, vmem_limit_bytes=63 << 20
@@ -1082,8 +1107,8 @@
     gain,
     shift,
     down_bias,
-    out_far,
-    out_own,
+    far_hbm,
+    own_hbm,
     grad_middle,
     grad_mixed,
     up_part,
@@ -1122,6 +1147,9 @@
     up,
     down,
     load_sems,
+    out_far,
+    out_own,
+    store_sems,
 ):
     team = Team()
     length = mixed_ref.shape[0]
@@ -1333,6 +1361,9 @@
 
     lax.fori_loop(0, steps // 2, pair_forward, 0)
     lax.fori_loop(0, steps // 2, pair_backward, 0)
+    stores = loads_of(((out_far, far_hbm), (out_own, own_hbm)), store_sems)
+    for store in stores:
+        store.start()
     side_half(0)
     add_side(1)
     down_total.start(0)
@@ -1393,6 +1424,8 @@
             exchange(index, slot, owner).wait()
     down_keep.wait()
     up_keep.wait()
+    for store in stores:
+        store.wait()
     for spread in spreads:
         spread.sent()
     for pair in (steps // 2 - 2, steps // 2 - 1):
@@ -1424,7 +1457,7 @@
             shape((8, width), FULL),
         ),
         in_specs=[ANY] * 7 + [VMEM] * 5,
-        out_specs=(VMEM,) * 4 + (ANY, ANY, VMEM, VMEM),
+        out_specs=(ANY, ANY, VMEM, VMEM, ANY, ANY, VMEM, VMEM),
         scratch_shapes=[
             pltpu.VMEM((own, width), FULL),
             pltpu.VMEM((width // 2, hidden), FULL),
@@ -1458,6 +1491,9 @@
             pltpu.VMEM(up.shape, LOW),
             pltpu.VMEM(down.shape, LOW),
             DMA((6,)),
+            pltpu.VMEM((own, width), LOW),
+            pltpu.VMEM((own, width), FULL),
+            DMA((2,)),
         ],
         compiler_params=pltpu.CompilerParams(
             collective_id=2, has_side_effects=True, vmem_limit_bytes=63 << 20

time: 282 us -> 280 us (level)
  Pallas kernels: 269 us -> 266 us
where the time goes in v3:
time: 280 us; the launch traced here: 279 us
  Pallas kernels  266 us (95%)
  local copies, waits for them, and re-layouts  8.03 us (3%)
  other arithmetic  4.46 us (2%)
    pallas_call x1, Pallas kernels, ffn(): pl.pallas_call(functools.partial(ffn_kernel, part, size), out_shape=(shap...  75.9 us
    pallas_call x1, Pallas kernels, attend_backward(): pl.pallas_call(functools.partial(backward_kernel, 256, 512, head_count, s...  60.7 us
    pallas_call x1, Pallas kernels, last(): pl.pallas_call(functools.partial(last_kernel, part, size), out_shape=(sha...  52.9 us
    pallas_call x1, Pallas kernels, attend_forward(): pl.pallas_call(functools.partial(forward_kernel, 256, 512, head_count), o...  45.4 us
    pallas_call x1, Pallas kernels, gather_and_project(): pl.pallas_call(functools.partial(project_kernel, part), out_shape=(wide,...  31.2 us

profile of v3, /device:TPU:0, one launch (start us, length us, event | category | flops | bytes accessed | tf_op | source)
XLA Modules:
  0.0 279.3 jit_solution(15696886002185129313)
XLA Ops:
  0.7 31.2 %gather_and_project.1 = (bf16[2560,768]{1,0:T(8,128)(2,1)}, bf16[2560,768]{1,0:T(8,128)(2,1)}, bf16[2560,192]{1,0:T(8,128)(2,1)}, bf16[2560,192]{1,0:T(8,128)(2,1)}, bf16[2560,192]{1,0:T(8,128)(2,1)}) custom-call(bf16[640,768]{1,0:T(8,128)(2,1)} %x_ref.1, bf16[768]{0:T(1024)(128)(2,1)} %gain.5, bf16[768]{0:T(1024)(128)(2,1)} %shift.2, ...), custom_call_target="tpu_custom_call" | custom-call | tf_op jit(solution)/shard_map/gather_and_project/pallas_call | solution.py:1009
  31.9 45.4 %attend_forward.1 = (bf16[2560,192]{1,0:T(8,128)(2,1)}, f32[392,8,192]{2,1,0:T(8,128)}, f32[2560,128]{1,0:T(8,128)}, bf16[3,2560,192]{2,1,0:T(8,128)(2,1)}, bf16...) custom-call(s32[1,2560]{1,0:T(1,128)} %spans.3, ...), custom_call_target="tpu_custom_call" | custom-call | tf_op jit(solution)/shard_map/attend_forward/pallas_call | solution.py:353
  77.3 75.9 %ffn.1 = (bf16[640,768]{1,0:T(8,128)(2,1)}, f32[640,768]{1,0:T(8,128)}, f32[640,768]{1,0:T(8,128)}, bf16[2560,192]{1,0:T(8,128)(2,1)}, f32[384,768]{1,0:T(8,128)...) custom-call(bf16[2560,192]{1,0:T(8,128)(2,1)} %get-tuple-element.51.mixed_hbm, ...), custom_call_target="tpu_custom_call" | custom-call | tf_op jit(solution)/shard_map/ffn/pallas_call | solution.py:1447
  153.1 60.7 %attend_backward.1 = (bf16[2560,192]{1,0:T(8,128)(2,1)}, bf16[2560,192]{1,0:T(8,128)(2,1)}, bf16[2560,192]{1,0:T(8,128)(2,1)}, bf16[768,768]{1,0:T(8,128)(2,1)},...) custom-call(s32[1,2560]{1,0:T(1,128)} %spans.3, ...), custom_call_target="tpu_custom_call" | custom-call | tf_op jit(solution)/shard_map/attend_backward/pallas_call | solution.py:844
  213.8 0.0 copy-start.2
  213.8 0.0 copy-start.5
  213.8 52.9 %last.1 = (f32[640,768]{1,0:T(8,128)}, bf16[768,768]{1,0:T(8,128)(2,1)}, f32[16,768]{1,0:T(8,128)}) custom-call(bf16[2560,192]{1,0:T(8,128)(2,1)} %get-tuple-element.67.dq_hbm, bf16[2560,192]{1,0:T(8,128)(2,1)} %get-tuple-element.68.dk_hbm, bf16[2560,192]{1,0:T(8,128)(2,1)} %get-tuple-element.69.dv_hbm, bf16[192,768]{1,0:T(8,128)(2,1)} %bitcast.12, ...), custom_call_target="tpu_custom_call" | custom-call | tf_op jit(solution)/shard_map/last/pallas_call | solution.py:1686
  266.7 0.0 copy-done.2
  266.7 0.0 copy-done.5
  266.7 0.0 copy-start
  266.8 1.1 add_convert_fusion
  267.9 1.3 fusion
  269.2 1.7 slice_reduce_fusion
  271.0 0.0 copy-done
  271.0 0.9 slice.55
  271.8 0.2 convert_element_type.17
  272.0 0.0 copy-start.4
  272.0 1.2 slice_bitcast_fusion
  273.3 0.7 copy-done.4
  273.9 0.0 copy-start.3
  273.9 1.6 convert_element_type.18
  275.5 0.1 copy-done.3
  275.6 0.0 copy-start.1
  275.6 1.6 convert_element_type.19
  277.2 0.8 copy-done.1
  278.0 1.3 copy.36
Async XLA Ops:
  213.8 52.9 %copy-start.2 = (f32[640,768]{1,0:T(8,128)S(1)}, f32[640,768]{1,0:T(8,128)}, u32[]{:S(2)}) copy-start(f32[640,768]{1,0:T(8,128)} %get-tuple-element.55) | copy-start | bytes 5898244
  213.8 52.9 %copy-start.5 = (bf16[640,768]{1,0:T(8,128)(2,1)S(1)}, bf16[640,768]{1,0:T(8,128)(2,1)}, u32[]{:S(2)}) copy-start(bf16[640,768]{1,0:T(8,128)(2,1)} %get-tuple-element.66) | copy-start | bytes 2949124
  266.7 4.2 %copy-start = (bf16[768,768]{1,0:T(8,128)(2,1)S(1)}, bf16[768,768]{1,0:T(8,128)(2,1)}, u32[]{:S(2)}) copy-start(bf16[768,768]{1,0:T(8,128)(2,1)} %get-tuple-element.76) | copy-start | bytes 3538948
  272.0 1.9 copy-start.4
  273.9 1.7 copy-start.3
  275.6 2.4 copy-start.1
